TPU v7x, 512 devices: a whole 4x8x8 slice. The times are simulated.
512 devices in a mesh: space: 64 (over z, y), batch: 8 (over x, core).
Axes of the slice: x: 4, y: 8, z: 8, core: 2. Of those that a mesh axis runs over, the one named last changes fastest.
Arguments:
- features: bfloat16 [8, 32768, 128], P('batch', 'space'), may hold values from -6 to 6
- weights: bfloat16 [27, 128, 128], replicated, may hold values from -0.109375 to 0.109375
- kernel_map: int32 [8, 27, 32768], P('batch', None, 'space'), may hold values from 0 to 768, as said below
- send_rows: int32 [8, 2, 8192], P('batch', None, 'space'), may hold values from 0 to 511, as said below
- counts: int32 [8, 64], P('batch', 'space'), may hold values from 64 to 512, as said below
- cotangent: bfloat16 [8, 32768, 128], P('batch', 'space'), may hold values from -6 to 6
Outputs:
- output: bfloat16 [8, 32768, 128], P('batch', 'space')
- grad_features: bfloat16 [8, 32768, 128], P('batch', 'space')
- grad_weights: float32 [27, 128, 128], replicated
Inputs may be any that keep to these rules, and one draw needn't show every extreme that they name: `kernel_map`: values below 512 are active slots of the same block (below its count); 512 to 639 are rows received from the lower block, the next 128 rows from the upper block, 768 is the zero row. The first block never reads the lower rows, the last never the upper ones. The middle offset reads each active slot itself; inactive slots read only the zero row. `send_rows`: every entry is an active slot of the sending block. `counts`: each scene tile has a block with all 512 slots active and a block with exactly 64; every block has at least 64.
All inputs are finite; a program needn't handle non-finite values.
Results may differ from a plain program's by a relative error of at most 0.001.
Values may be sent and summed in bfloat16 or wider, within the bound.
No kernel may reach another device: no remote copies, remote signals or barrier semaphores. Data moves between devices by JAX's collectives and lax.ppermute only.
A program may use at most 64 MiB of HBM per device.

v0:
```python
import jax
import jax.numpy as jnp
from jax import lax
from jax.sharding import PartitionSpec as P


def with_halo(shard, sides, width):
    for axis, dim in sides:
        size, length = (lax.axis_size(axis), shard.shape[dim])
        up = [(i, (i + 1) % size) for i in range(size - 1)]
        down = [(j, i) for i, j in up]
        last = lax.slice_in_dim(shard, length - width, length, axis=dim)
        first = lax.slice_in_dim(shard, 0, width, axis=dim)
        before = lax.ppermute(last, axis, up)
        after = lax.ppermute(first, axis, down)
        shard = jnp.concatenate([before, shard, after], axis=dim)
    return shard


def per_device(features, weights, kernel_map, send_rows, counts, cotangent):
    slots = features.shape[1]
    channels = features.shape[2]
    offsets = weights.shape[0]
    alive = (lax.iota(jnp.int32, slots) < counts[0, 0])[:, None]
    live = jnp.where(alive, features[0], jnp.zeros((), jnp.bfloat16))
    zero_row = jnp.zeros((1, channels), jnp.bfloat16)
    padded = jnp.concatenate([live, zero_row], 0)
    send_lists = send_rows[0]
    halo_width = send_lists.shape[1]
    outgoing = padded[send_lists]
    beside_all = with_halo(outgoing, (("space", 0),), 1)
    extended = jnp.concatenate([live, beside_all[0], beside_all[3], zero_row], 0)
    offset_map = kernel_map[0]

    def forward_step(running, pair):
        source, weight = pair
        return (
            running + jnp.dot(extended[source], weight, preferred_element_type=jnp.float32),
            None,
        )

    result, unused = lax.scan(
        forward_step, jnp.zeros((slots, channels), jnp.float32), (offset_map, weights)
    )
    output = jnp.where(alive, result, jnp.zeros((), jnp.float32)).astype(jnp.bfloat16)
    grad_rows = jnp.where(alive, cotangent[0], jnp.zeros((), jnp.bfloat16))

    def backward_step(accum_grad, pair):
        source, weight = pair
        gathered = extended[source]
        weight_part = lax.dot_general(
            gathered, grad_rows, (((0,), (0,)), ((), ())), preferred_element_type=jnp.float32
        )
        contrib = jnp.dot(grad_rows, weight.T, preferred_element_type=jnp.float32)
        return (accum_grad.at[source].add(contrib), weight_part)

    ext_length = slots + 2 * halo_width + 1
    ext_grad, weight_parts = lax.scan(
        backward_step, jnp.zeros((ext_length, channels), jnp.float32), (offset_map, weights)
    )
    halo_grads = jnp.stack(
        [
            ext_grad[slots : slots + halo_width],
            ext_grad[slots + halo_width : slots + 2 * halo_width],
        ],
        0,
    )
    returned = with_halo(halo_grads, (("space", 0),), 1)
    local_grads = jnp.concatenate([ext_grad[:slots], jnp.zeros((1, channels), jnp.float32)], 0)
    local_grads = local_grads.at[send_lists[1]].add(returned[3]).at[send_lists[0]].add(returned[0])
    grad_features = jnp.where(alive, local_grads[:slots], jnp.zeros((), jnp.float32)).astype(
        jnp.bfloat16
    )
    flat_parts = weight_parts.reshape(offsets * channels, channels)
    summed = lax.psum(flat_parts, ("space", "batch"))
    total_rows = slots * lax.axis_size("space") * lax.axis_size("batch")
    grad_weights = (summed * total_rows ** (-0.5)).reshape(offsets, channels, channels)
    return (output[None], grad_features[None], grad_weights)


def solution(mesh):
    in_specs = (
        P("batch", "space", None),
        P(),
        P("batch", None, "space"),
        P("batch", None, "space"),
        P("batch", "space"),
        P("batch", "space", None),
    )
    out_specs = (P("batch", "space", None), P("batch", "space", None), P())
    return jax.shard_map(
        per_device, mesh=mesh, in_specs=in_specs, out_specs=out_specs, check_vma=False
    )
```

profile of v0, /device:TPU:1, one launch (start us, length us, event | category | flops | bytes accessed | tf_op | source)
XLA Modules:
  0.0 523.2 jit_solution(3977993782026609734)
XLA Ops:
  10.5 4.0 collective-permute-start
  19.5 187.1 %while.23 = (s32[]{:T(128)}, f32[769,128]{1,0:T(8,128)S(1)}, f32[27,128,128]{2,1,0:T(8,128)}, s32[27,512]{1,0:T(8,128)S(1)}, bf16[27,128,128]{2,1,0:T(8,128)(2,1...) while((s32[]{:T(128)}, f32[769,128]{1,0:T(8,128)S(1)}, ...), condition=%wide.region_4.5_spmd, body=%wide.region_2.4_spmd.sunk | while | flops 33622528 | bytes 2341977 | solution.py:58
  22.8 3.6 scatter_fusion
  29.7 3.6 scatter_fusion
  36.6 3.6 scatter_fusion
  43.6 3.6 scatter_fusion
  50.5 3.6 scatter_fusion
  57.4 3.6 scatter_fusion
  64.4 3.6 scatter_fusion
  71.3 3.6 scatter_fusion
  78.2 3.6 scatter_fusion
  85.2 3.6 scatter_fusion
  92.1 3.6 scatter_fusion
  99.0 3.6 scatter_fusion
  106.0 3.6 scatter_fusion
  112.9 3.6 scatter_fusion
  119.8 3.6 scatter_fusion
  126.8 3.6 scatter_fusion
  133.7 3.6 scatter_fusion
  140.6 3.6 scatter_fusion
  147.5 3.6 scatter_fusion
  154.5 3.6 scatter_fusion
  161.4 3.6 scatter_fusion
  168.3 3.6 scatter_fusion
  175.3 3.6 scatter_fusion
  182.2 3.6 scatter_fusion
  189.1 3.6 scatter_fusion
  196.0 3.6 scatter_fusion
  203.0 3.6 scatter_fusion
  207.9 8.4 %collective-permute-start.3 = (f32[1,128,128]{2,1,0:T(8,128)S(1)}, f32[1,128,128]{2,1,0:T(8,128)S(1)}, u32[]{:S(2)}, u32[]{:S(2)}) collective-permute-start(f32[1,128,128]{2,1,0:T(8,128)S(1)} %get-tuple-element.113), channel_id=1, source_target_pairs={{0,8},{8,16},{16,24},{24,32},{32,40},{40,48},{48,56},{56,64},{64,7... | collective-permute-start | bytes 196616 | tf_op jit(solution)/shard_map/ppermute | solution.py:14
  216.3 64.0 %while.24 = (s32[]{:T(128)}, f32[512,128]{1,0:T(8,128)S(1)}, s32[27,512]{1,0:T(8,128)S(1)}, bf16[769,128]{1,0:T(8,128)(2,1)S(1)}, bf16[27,128,128]{2,1,0:T(8,128)(2,1)}, /*index=5*/s32[]{:T(128)}, s32[]{:T(128)}) while((s32[]{:T(128)}, f32[512,128]{1,0:T(8,128)S(1)}, s32[27,512]{1,0:T(8,128)S(1)}, bf16[769,128]{1,0:T(8,128)(2,1)S(1)}, ...), condition=%wide.region_1.2_spmd.clone, body=%wide.region_0.1_spmd.clone.sunk | while | flops 16910852 | bytes 963163 | solution.py:42
  284.0 229.6 %all-reduce.3.cloned.1.call-done = f32[3456,128]{1,0:T(8,128)} async-done(((f32[3456,128]{1,0:T(8,128)}), f32[3456,128]{1,0:T(8,128)}) %all-reduce.3.cloned.1.call-update) | async-done | bytes 1769488 | tf_op jit(solution)/shard_map/psum | solution.py:75
  (300 shorter events, 166.6 us)
Async XLA Ops:
  7.2 506.4 %all-reduce.3.cloned.1.call-start = ((), (), s32[]{:S(2)}) async-start(), calls=%async_computation | async-start | bytes 3538944 | tf_op jit(solution)/shard_map/psum | solution.py:75
  10.5 6.9 %collective-permute-start = (bf16[1,128,128]{2,1,0:T(8,128)(2,1)S(1)}, bf16[1,128,128]{2,1,0:T(8,128)(2,1)S(1)}, u32[]{:S(2)}, u32[]{:S(2)}) collective-permute-start(bf16[1,128,128]{2,1,0:T(8,128)(2,1)S(1)} %get-tuple-element.115), channel_id=1, source_target_pairs={{0,8},{8,16},{16,24},{24,32},{32,40},{40,48},{48,56},{56,64},{64,7... | collective-permute-start | bytes 98312 | tf_op jit(solution)/shard_map/ppermute | solution.py:14
  14.6 4.7 collective-permute-start.1
  206.6 73.9 %collective-permute-start.2 = (f32[1,128,128]{2,1,0:T(8,128)S(1)}, f32[1,128,128]{2,1,0:T(8,128)S(1)}, u32[]{:S(2)}, u32[]{:S(2)}) collective-permute-start(f32[1,128,128]{2,1,0:T(8,128)S(1)} %get-tuple-element.114), channel_id=1, source_target_pairs={{8,0},{16,8},{24,16},{32,24},{40,32},{48,40},{56,48},{64,56},{72,6... | collective-permute-start | bytes 196616 | tf_op jit(solution)/shard_map/ppermute | solution.py:15
  207.9 74.0 %collective-permute-start.3 = (f32[1,128,128]{2,1,0:T(8,128)S(1)}, f32[1,128,128]{2,1,0:T(8,128)S(1)}, u32[]{:S(2)}, u32[]{:S(2)}) collective-permute-start(f32[1,128,128]{2,1,0:T(8,128)S(1)} %get-tuple-element.113), channel_id=1, source_target_pairs={{0,8},{8,16},{16,24},{24,32},{32,40},{40,48},{48,56},{56,64},{64,7... | collective-permute-start | bytes 196616 | tf_op jit(solution)/shard_map/ppermute | solution.py:14
  216.3 64.1 %copy-start = (pred[513]{0:T(1024)(128)(4,1)S(1)}, pred[513]{0:T(1024)(128)(4,1)}, u32[]{:S(2)}) copy-start(pred[513]{0:T(1024)(128)(4,1)} %constant.26.clone.1) | copy-start | bytes 1543
Sparse Core Ops, SparseCore 0:
  216.4 297.1 all-reduce.2
where the time goes:
time: 527 us; the launch traced here: 523 us
  waiting for transfers between devices  231 us (44%)
  other arithmetic  107 us (20%)
  local copies, waits for them, and re-layouts  77.3 us (15%)
  matrix products  74.8 us (14%)
  starting transfers between devices  15 us (3%)
  between operations  14.8 us (3%)
    psum x1, waiting for transfers between devices, per_device(): summed = lax.psum(flat_parts, ('space', 'batch'))  230 us
    scatter-add x27, other arithmetic, backward_step(): return (accum_grad.at[source].add(contrib), weight_part)  96.8 us
    gather x27, local copies, waits for them, and re-layouts, backward_step(): gathered = extended[source]  36.2 us
    gather x27, local copies, waits for them, and re-layouts, forward_step(): extended[source]  36.2 us
    dot_general x27, matrix products, forward_step(): jnp.dot(extended[source], weight, preferred_element_type=jnp.float32)  26 us
    dot_general x27, matrix products, backward_step(): contrib = jnp.dot(grad_rows, weight.T, preferred_element_type=jnp.float32)  25.4 us
    dot_general x27, matrix products, backward_step(): lax.dot_general(gathered, grad_rows, (((0,), (0,)), ((), ())), preferred_...  23.3 us
    ppermute x2, starting transfers between devices, with_halo(): before = lax.ppermute(last, axis, up)  12.4 us
  transfers between devices with their start and end apart: 5, of which 2 were waited for; matrix products, arithmetic and copies ran while one was open for 13% of the time, Pallas kernels for 0%

commit v1 on v0

v1 whole, which is shorter than its diff:
```python
import jax
import jax.numpy as jnp
from jax import lax
from jax.experimental import pallas as pl
from jax.experimental.pallas import tpu as pltpu
from jax.sharding import Mesh, PartitionSpec as P

C = 128
KV = 27
VOX = 512
HALO = 128
EXT = VOX + 2 * HALO
SCALE = 262144**-0.5
VMEM_LIMIT = 48 * 2**20

f32 = jnp.float32
bf16 = jnp.bfloat16


def onehot(indices, rows):
    line = lax.broadcasted_iota(jnp.int32, (rows, indices.shape[1]), 0)
    return jnp.where(line == indices, jnp.ones((), bf16), jnp.zeros((), bf16))


def masked(count, values):
    alive = lax.broadcasted_iota(jnp.int32, values.shape, 0) < count[0, 0]
    return jnp.where(alive, values, jnp.zeros((), values.dtype))


def split(values):
    high = values.astype(bf16)
    low = (values - high.astype(f32)).astype(bf16)
    return jnp.concatenate([high, low], axis=1)


def joined(both):
    return both[:, :C] + both[:, C:]


def matmul(a, b, dims=((1,), (0,))):
    return lax.dot_general(a, b, (dims, ((), ())), preferred_element_type=f32)


def pick_kernel(count, features, send, outgoing):
    live = masked(count, features[...])
    for side in range(2):
        rows = onehot(send[side : side + 1, :], VOX)
        outgoing[side] = matmul(rows, live, ((0,), (0,))).astype(bf16)


def scatter_kernel(count, cotangent, weights, kernel_map, ext_grad, grad_rows, acc):
    grad_rows[...] = masked(count, cotangent[...])
    acc[...] = jnp.zeros_like(acc)
    for k in range(KV):
        contrib = matmul(grad_rows[...], weights[k], ((1,), (1,)))
        acc[...] += matmul(onehot(kernel_map[k : k + 1, :], EXT), split(contrib))
    ext_grad[...] = joined(acc[...])


def gather_kernel(
    count, features, lower, upper, weights, kernel_map, grad_rows, output, weight_grad, table, gathered
):
    table[:, :VOX] = masked(count, features[...]).T
    table[:, VOX : VOX + HALO] = lower[...].T
    table[:, VOX + HALO :] = upper[...].T
    for k in range(KV):
        rows = onehot(kernel_map[k : k + 1, :], EXT)
        gathered[k * C : (k + 1) * C, :] = matmul(table[...], rows).astype(bf16)
    weight_grad[...] = matmul(gathered[...], grad_rows[...]) * SCALE
    result = matmul(weights[...].reshape(KV * C, C), gathered[...], ((0,), (0,)))
    output[...] = masked(count, result.T).astype(bf16)


def finish_kernel(count, ext_grad, for_upper, for_lower, send, grad_features):
    total = ext_grad[:VOX, :]
    for side, returned in ((1, for_upper), (0, for_lower)):
        rows = onehot(send[side : side + 1, :], VOX)
        total = total + joined(matmul(rows, split(returned[...])))
    grad_features[...] = masked(count, total).astype(bf16)


def call(kernel, name, args, outs, scratch=(), flops=0):
    scalar = pl.BlockSpec(memory_space=pltpu.SMEM)
    vector = pl.BlockSpec(memory_space=pltpu.VMEM)
    outs = tuple(jax.ShapeDtypeStruct(*o) for o in outs)
    moved = sum(a.size * a.dtype.itemsize for a in (*args, *outs))
    return pl.pallas_call(
        kernel,
        name=name,
        in_specs=[scalar] + [vector] * (len(args) - 1),
        out_specs=(vector,) * len(outs),
        out_shape=outs,
        scratch_shapes=[pltpu.VMEM(*s) for s in scratch],
        cost_estimate=pl.CostEstimate(flops=flops, transcendentals=0, bytes_accessed=moved),
        compiler_params=pltpu.CompilerParams(vmem_limit_bytes=VMEM_LIMIT),
    )(*args)


def exchange(parts, axes):
    return lax.all_to_all(parts, axes, 0, 0, tiled=False)


def spread(part, axes, size):
    return exchange(jnp.broadcast_to(part[None], (size, *part.shape)), axes).reshape(-1, C)


def mesh_sum(values):
    half = exchange(values.reshape(2, -1, C), "c").sum(0)
    part = exchange(half.reshape(4, -1, C), "x").sum(0)
    rows = part.shape[0]
    padded = jnp.pad(part, ((0, -rows % (64 * 8)), (0, 0)))
    piece = exchange(padded.reshape(64, -1, C), ("z", "y")).sum(0)
    part = spread(piece, ("z", "y"), 64)[:rows]
    return spread(spread(part, "x", 4), "c", 2)


def per_device(features, weights, kernel_map, send_rows, counts, cotangent):
    features, kernel_map, send, cotangent = features[0], kernel_map[0], send_rows[0], cotangent[0]
    space = ("z", "y")
    size = lax.axis_size(space)
    up = [(i, i + 1) for i in range(size - 1)]
    down = [(i + 1, i) for i in range(size - 1)]
    (outgoing,) = call(pick_kernel, "pick", (counts, features, send), [((2, HALO, C), bf16)])
    lower_in = lax.ppermute(outgoing[1], space, up)
    upper_in = lax.ppermute(outgoing[0], space, down)
    ext_grad, grad_rows = call(
        scatter_kernel,
        "scatter",
        (counts, cotangent, weights, kernel_map),
        [((EXT, C), f32), ((VOX, C), bf16)],
        [((EXT, 2 * C), f32)],
        2 * KV * VOX * C * (C + 2 * EXT),
    )
    for_lower = lax.ppermute(ext_grad[VOX + HALO :], space, up)
    for_upper = lax.ppermute(ext_grad[VOX : VOX + HALO], space, down)
    output, weight_grad = call(
        gather_kernel,
        "gather",
        (counts, features, lower_in, upper_in, weights, kernel_map, grad_rows),
        [((VOX, C), bf16), ((KV * C, C), f32)],
        [((C, EXT), bf16), ((KV * C, VOX), bf16)],
        2 * KV * VOX * C * (2 * C + EXT),
    )
    (grad_features,) = call(
        finish_kernel,
        "finish",
        (counts, ext_grad, for_upper, for_lower, send),
        [((VOX, C), bf16)],
    )
    grad_weights = mesh_sum(weight_grad).reshape(KV, C, C)
    return output[None], grad_features[None], grad_weights


def solution(mesh):
    fine = Mesh(mesh.devices.reshape(8, 8, 4, 2), ("z", "y", "x", "c"))
    space, batch = ("z", "y"), ("x", "c")
    in_specs = (
        P(batch, space, None),
        P(),
        P(batch, None, space),
        P(batch, None, space),
        P(batch, space),
        P(batch, space, None),
    )
    out_specs = (P(batch, space, None), P(batch, space, None), P())
    return jax.shard_map(
        per_device, mesh=fine, in_specs=in_specs, out_specs=out_specs, check_vma=False
    )
```

time: 527 us -> 126 us (0.24)
  waiting for transfers between devices: 231 us -> 4.36 us
  other arithmetic: 107 us -> 0.3 us
  blocking collectives: 0 us -> 78.2 us
  matrix products: 74.8 us -> 0 us
  local copies, waits for them, and re-layouts: 77.3 us -> 6.84 us
  Pallas kernels: 0 us -> 20.2 us
  between operations: 14.8 us -> 1.41 us
    psum x1 -> x0, waiting for transfers between devices: 230 us -> none  [per_device(): summed = lax.psum(flat_parts, ('space', 'batch'))]
    scatter-add x29 -> x0, other arithmetic: 99.4 us -> none  [the longest x27 96.8 us: backward_step(): return (accum_grad.at[source].add(contrib), weight_part)]
    all_to_all x0 -> x5, blocking collectives: none -> 78.2 us  [exchange(): return lax.all_to_all(parts, axes, 0, 0, tiled=False)]
    dot_general x81 -> x0, matrix products: 74.8 us -> none  [the longest x27 26 us: forward_step(): jnp.dot(extended[source], weight, preferred_element_type=jnp.float32)]
    gather x55 -> x0, local copies, waits for them, and re-layouts: 73.2 us -> none  [the longest x27 36.2 us: backward_step(): gathered = extended[source]]
    pallas_call x0 -> x4, Pallas kernels: none -> 20.2 us  [call(): pl.pallas_call(kernel, name=name, in_specs=[scalar] + [vector] * (len(arg...]
  transfers between devices with their start and end apart: 5 -> 5, of which waited for: 2 -> 2; matrix products, arithmetic and copies ran while one was open for 13% -> 1% of each run, Pallas kernels for 0% -> 11%
where the time goes in v1:
time: 126 us; the launch traced here: 125 us
  blocking collectives  78.2 us (62%)
  Pallas kernels  20.2 us (16%)
  starting transfers between devices  13.6 us (11%)
  local copies, waits for them, and re-layouts  6.84 us (5%)
  waiting for transfers between devices  4.36 us (3%)
  between operations  1.41 us (1%)
    all_to_all x5, blocking collectives, exchange(): return lax.all_to_all(parts, axes, 0, 0, tiled=False)  78.2 us
    pallas_call x4, Pallas kernels, call(): pl.pallas_call(kernel, name=name, in_specs=[scalar] + [vector] * (len(arg...  20.2 us
    unnamed x14, local copies, waits for them, and re-layouts  5.68 us
    ppermute x1, starting transfers between devices, per_device(): lower_in = lax.ppermute(outgoing[1], space, up)  4.66 us
    ppermute x1, waiting for transfers between devices, per_device(): for_upper = lax.ppermute(ext_grad[VOX:VOX + HALO], space, down)  3.99 us
    all_to_all x1, starting transfers between devices, exchange(): return lax.all_to_all(parts, axes, 0, 0, tiled=False)  3.5 us
    ppermute x1, starting transfers between devices, per_device(): for_lower = lax.ppermute(ext_grad[VOX + HALO:], space, up)  2.88 us
  transfers between devices with their start and end apart: 5, of which 2 were waited for; matrix products, arithmetic and copies ran while one was open for 1% of the time, Pallas kernels for 11%

profile of v1, /device:TPU:1, one launch (start us, length us, event | category | flops | bytes accessed | tf_op | source)
XLA Modules:
  0.0 125.0 jit_solution(7994448191039345066)
XLA Ops:
  1.3 0.0 copy-start
  1.3 0.9 copy-done
  2.2 0.7 copy-done.2
  2.9 0.3 pick.1
  3.2 1.3 %collective-permute-start.1 = (bf16[128,128]{1,0:T(8,128)(2,1)S(1)}, bf16[128,128]{1,0:T(8,128)(2,1)S(1)}, u32[]{:S(2)}, u32[]{:S(2)}) collective-permute-start(bf16[128,128]{1,0:T(8,128)(2,1)S(1)} %get-tuple-element.13), channel_id=1, source_target_pairs={{8,0},{16,8},{24,16},{32,24},{40,32},{48,40},{56,48},{64,56},{72,6... | collective-permute-start | bytes 98312 | tf_op jit(solution)/shard_map/ppermute | solution.py:125
  4.5 4.7 %collective-permute-start = (bf16[128,128]{1,0:T(8,128)(2,1)S(1)}, bf16[128,128]{1,0:T(8,128)(2,1)S(1)}, u32[]{:S(2)}, u32[]{:S(2)}) collective-permute-start(bf16[128,128]{1,0:T(8,128)(2,1)S(1)} %get-tuple-element.14), channel_id=1, source_target_pairs={{0,8},{8,16},{16,24},{24,32},{32,40},{40,48},{48,56},{56,64},{64,7... | collective-permute-start | bytes 98312 | tf_op jit(solution)/shard_map/ppermute | solution.py:124
  9.2 0.8 copy.11
  10.0 1.2 copy-done.4
  11.2 0.9 copy-done.5
  12.1 12.9 %scatter.1 = (f32[768,128]{1,0:T(8,128)S(1)}, bf16[512,128]{1,0:T(8,128)(2,1)S(1)}) custom-call(s32[1,1]{1,0:T(1,128)S(6)} %copy.13.count, bf16[512,128]{1,0:T(8,128)(2,1)S(1)} %bitcast.27, bf16[27,128,128]{2,1,0:T(8,128)(2,1)S(1)} %copy-done.4, s32[27,512]{1,0:T(8,128)S(1)} %bitcast.23), custom_call_target="tpu_custom_call" | custom-call | flops 5888802816 | bytes 1595396 | tf_op jit(solution)/shard_map/scatter/pallas_call | solution.py:87
  25.0 0.0 collective-permute-done.1.upper
  25.0 0.0 collective-permute-done.lower
  25.0 0.0 copy-done.1
  25.0 6.1 %gather.1 = (bf16[512,128]{1,0:T(8,128)(2,1)}, f32[3456,128]{1,0:T(8,128)S(1)}) custom-call(s32[1,1]{1,0:T(1,128)S(6)} %copy.13.count, bf16[512,128]{1,0:T(8,128)(2,1)S(1)} %bitcast.22, bf16[128,128]{1,0:T(8,128)(2,1)S(1)} %collective-permute-done.lower, bf16[128,128]{1,0:T(8,128)(2,1)S(1)} %collective-permute-done.1.upper, ...), custom_call_target="tpu_custom_call" | custom-call | flops 3623878656 | bytes 3168260 | tf_op jit(solution)/shard_map/gather/pallas_call | solution.py:87
  31.1 11.5 %all_to_all.30 = f32[2,1728,128]{2,1,0:T(8,128)S(1)} all-to-all(f32[2,1728,128]{2,1,0:T(8,128)S(1)} %bitcast.20), channel_id=1, replica_groups=mesh['z'=8,'y'=8,'x'=4,'c'=2] {'c'}, dimensions={0} | all-to-all | bytes 3538944 | tf_op jit(solution)/shard_map/all_to_all | solution.py:100
  42.6 0.2 reduce_sum.27
  42.8 15.5 %all_to_all.31 = f32[4,432,128]{2,1,0:T(8,128)S(1)} all-to-all(f32[4,432,128]{2,1,0:T(8,128)S(1)} %bitcast.29), channel_id=1, replica_groups=mesh['z'=8,'y'=8,'x'=4,'c'=2] {'x'}, dimensions={0} | all-to-all | bytes 1769472 | tf_op jit(solution)/shard_map/all_to_all | solution.py:100
  58.4 24.2 %all_to_all.32 = f32[64,8,128]{2,1,0:T(8,128)S(1)} all-to-all(f32[64,8,128]{2,1,0:T(8,128)S(1)} %pad_bitcast_fusion), channel_id=1, replica_groups=mesh['z'=8,'y'=8,'x'=4,'c'=2] {'z','y'}, dimensions={0} | all-to-all | bytes 524288 | tf_op jit(solution)/shard_map/all_to_all | solution.py:100
  82.6 0.1 reduce_sum.29
  82.7 17.4 %all_to_all.33 = f32[64,8,128]{2,1,0:T(8,128)S(1)} all-to-all(f32[64,8,128]{2,1,0:T(8,128)S(1)} %broadcast_in_dim.29), channel_id=1, replica_groups=mesh['z'=8,'y'=8,'x'=4,'c'=2] {'z','y'}, dimensions={0} | all-to-all | bytes 524288 | tf_op jit(solution)/shard_map/all_to_all | solution.py:100
  100.1 1.0 broadcast_in_dim.31
  101.1 3.5 %all-to-all-start.4 = ((f32[4,432,128]{2,1,0:T(8,128)}), f32[4,432,128]{2,1,0:T(8,128)S(1)}, u32[]{:S(2)}, u32[]{:S(2)}) async-start(f32[4,432,128]{2,1,0:T(8,128)} %broadcast_in_dim.31), calls=%async_computation.4 | async-start | bytes 1769472 | tf_op jit(solution)/shard_map/all_to_all | solution.py:100
  104.6 2.9 %collective-permute-start.3 = (f32[128,128]{1,0:T(8,128)S(1)}, f32[128,128]{1,0:T(8,128)S(1)}, u32[]{:S(2)}, u32[]{:S(2)}) collective-permute-start(f32[128,128]{1,0:T(8,128)S(1)} %get-tuple-element.11), channel_id=1, source_target_pairs={{0,8},{8,16},{16,24},{24,32},{32,40},{40,48},{48,56},{56,64},{64,7... | collective-permute-start | bytes 196616 | tf_op jit(solution)/shard_map/ppermute | solution.py:134
  107.5 1.3 %collective-permute-start.2 = (f32[128,128]{1,0:T(8,128)S(1)}, f32[128,128]{1,0:T(8,128)S(1)}, u32[]{:S(2)}, u32[]{:S(2)}) collective-permute-start(f32[128,128]{1,0:T(8,128)S(1)} %get-tuple-element.12), channel_id=1, source_target_pairs={{8,0},{16,8},{24,16},{32,24},{40,32},{48,40},{56,48},{64,56},{72,6... | collective-permute-start | bytes 196616 | tf_op jit(solution)/shard_map/ppermute | solution.py:135
  108.8 0.0 collective-permute-done.3.for_lower
  108.8 4.0 %collective-permute-done.2.for_upper = f32[128,128]{1,0:T(8,128)S(1)} collective-permute-done((f32[128,128]{1,0:T(8,128)S(1)}, f32[128,128]{1,0:T(8,128)S(1)}, u32[]{:S(2)}, u32[]{:S(2)}) %collective-permute-start.2) | collective-permute-done | bytes 65568 | tf_op jit(solution)/shard_map/ppermute | solution.py:135
  112.8 0.0 copy-done.3
  112.8 0.9 finish.1
  113.8 0.3 all-to-all-done.4
  114.1 0.1 broadcast_in_dim.33
  114.2 9.5 %all_to_all.34 = f32[2,1728,128]{2,1,0:T(8,128)S(1)} all-to-all(f32[2,1728,128]{2,1,0:T(8,128)S(1)} %broadcast_in_dim.33), channel_id=1, replica_groups=mesh['z'=8,'y'=8,'x'=4,'c'=2] {'c'}, dimensions={0} | all-to-all | bytes 3538944 | tf_op jit(solution)/shard_map/all_to_all | solution.py:100
  123.8 1.2 copy.14
  (11 shorter events, 0.1 us)
Async XLA Ops:
  1.3 0.9 copy-start
  2.2 0.7 copy-start.2
  3.2 21.8 %collective-permute-start.1 = (bf16[128,128]{1,0:T(8,128)(2,1)S(1)}, bf16[128,128]{1,0:T(8,128)(2,1)S(1)}, u32[]{:S(2)}, u32[]{:S(2)}) collective-permute-start(bf16[128,128]{1,0:T(8,128)(2,1)S(1)} %get-tuple-element.13), channel_id=1, source_target_pairs={{8,0},{16,8},{24,16},{32,24},{40,32},{48,40},{56,48},{64,56},{72,6... | collective-permute-start | bytes 98312 | tf_op jit(solution)/shard_map/ppermute | solution.py:125
  4.5 20.5 %collective-permute-start = (bf16[128,128]{1,0:T(8,128)(2,1)S(1)}, bf16[128,128]{1,0:T(8,128)(2,1)S(1)}, u32[]{:S(2)}, u32[]{:S(2)}) collective-permute-start(bf16[128,128]{1,0:T(8,128)(2,1)S(1)} %get-tuple-element.14), channel_id=1, source_target_pairs={{0,8},{8,16},{16,24},{24,32},{32,40},{40,48},{48,56},{56,64},{64,7... | collective-permute-start | bytes 98312 | tf_op jit(solution)/shard_map/ppermute | solution.py:124
  10.0 1.2 copy-start.4
  11.2 0.9 copy-start.5
  12.1 12.9 %copy-start.1 = (bf16[1,512,128]{2,1,0:T(8,128)(2,1)S(1)}, bf16[1,512,128]{2,1,0:T(8,128)(2,1)}, u32[]{:S(2)}) copy-start(bf16[1,512,128]{2,1,0:T(8,128)(2,1)} %param.6) | copy-start | bytes 393220
  100.1 12.7 %copy-start.3 = (s32[1,2,128]{2,1,0:T(2,128)S(1)}, s32[1,2,128]{2,1,0:T(2,128)}, u32[]{:S(2)}) copy-start(s32[1,2,128]{2,1,0:T(2,128)} %param.9) | copy-start | bytes 3076
  101.1 13.0 %all-to-all-start.4 = ((f32[4,432,128]{2,1,0:T(8,128)}), f32[4,432,128]{2,1,0:T(8,128)S(1)}, u32[]{:S(2)}, u32[]{:S(2)}) async-start(f32[4,432,128]{2,1,0:T(8,128)} %broadcast_in_dim.31), calls=%async_computation.4 | async-start | bytes 1769472 | tf_op jit(solution)/shard_map/all_to_all | solution.py:100
  104.6 4.2 %collective-permute-start.3 = (f32[128,128]{1,0:T(8,128)S(1)}, f32[128,128]{1,0:T(8,128)S(1)}, u32[]{:S(2)}, u32[]{:S(2)}) collective-permute-start(f32[128,128]{1,0:T(8,128)S(1)} %get-tuple-element.11), channel_id=1, source_target_pairs={{0,8},{8,16},{16,24},{24,32},{32,40},{40,48},{48,56},{56,64},{64,7... | collective-permute-start | bytes 196616 | tf_op jit(solution)/shard_map/ppermute | solution.py:134
  107.5 5.3 %collective-permute-start.2 = (f32[128,128]{1,0:T(8,128)S(1)}, f32[128,128]{1,0:T(8,128)S(1)}, u32[]{:S(2)}, u32[]{:S(2)}) collective-permute-start(f32[128,128]{1,0:T(8,128)S(1)} %get-tuple-element.12), channel_id=1, source_target_pairs={{8,0},{16,8},{24,16},{32,24},{40,32},{48,40},{56,48},{64,56},{72,6... | collective-permute-start | bytes 196616 | tf_op jit(solution)/shard_map/ppermute | solution.py:135

commit v2 on v1

v2 whole, which is shorter than its diff:
```python
import functools

import jax
import jax.numpy as jnp
from jax import lax
from jax.experimental import pallas as pl
from jax.experimental.pallas import tpu as pltpu
from jax.sharding import Mesh, PartitionSpec as P

C = 128
KV = 27
VOX = 512
HALO = 128
EXT = VOX + 2 * HALO
SCALE = 262144**-0.5
HALF = KV * C // 2
QUARTER = HALF // 4
CODED = QUARTER + 16
GROUP = 3
FIRST = 6
TILE = 256
VMEM_LIMIT = 16 * 2**20

f32 = jnp.float32
bf16 = jnp.bfloat16


def onehot(indices, rows, first=0):
    line = lax.broadcasted_iota(jnp.int32, (rows, indices.shape[1]), 0) + first
    return jnp.where(line == indices, jnp.ones((), bf16), jnp.zeros((), bf16))


def offset_onehot(kernel_map, k, rows, first=0):
    return onehot(kernel_map[k : k + 1, :], rows, first)


def masked(count, values):
    alive = lax.broadcasted_iota(jnp.int32, values.shape, 0) < count[0, 0]
    return jnp.where(alive, values, jnp.zeros((), values.dtype))


def split(values):
    high = values.astype(bf16)
    low = (values - high.astype(f32)).astype(bf16)
    return jnp.concatenate([high, low], axis=1)


def joined(both):
    return both[:, :C] + both[:, C:]


def matmul(a, b, dims=((1,), (0,))):
    return lax.dot_general(a, b, (dims, ((), ())), preferred_element_type=f32)


def pick_kernel(count, features, send, to_lower, to_upper):
    live = masked(count, features[...])
    for side, outgoing in ((0, to_lower), (1, to_upper)):
        rows = onehot(send[side : side + 1, :], VOX)
        outgoing[...] = matmul(rows, live, ((0,), (0,))).astype(bf16)


def local_kernel(count, features, kernel_map, gathered, table):
    table[...] = masked(count, features[...]).T
    for k in range(KV):
        rows = offset_onehot(kernel_map, k, VOX)
        gathered[k * C : (k + 1) * C, :] = matmul(table[...], rows).astype(bf16)


def halo_kernel(
    count, lower, upper, kernel_map, own, cotangent, kept, sent, gathered, grad_rows, table
):
    table[:, :HALO] = lower[...].T
    table[:, HALO:] = upper[...].T
    grad_rows[...] = masked(count, cotangent[...])
    for k in range(KV):
        rows = offset_onehot(kernel_map, k, 2 * HALO, VOX)
        part = slice(k * C, (k + 1) * C)
        gathered[part, :] = own[part, :] + matmul(table[...], rows).astype(bf16)
    first_core = lax.axis_index("c") == 0
    for row in range(0, HALF, HALF // 9):
        parts = [slice(row + start, row + start + HALF // 9) for start in (0, HALF)]
        low, high = (matmul(gathered[part, :], grad_rows[...]) * SCALE for part in parts)
        kept[parts[0], :] = jnp.where(first_core, low, high)
        sent[parts[0], :] = jnp.where(first_core, high, low)


def scatter_kernel(offsets, grad_rows, weights, kernel_map, *refs):
    *earlier, ext_grad, contribs = refs
    for first in range(*offsets, GROUP):
        group = range(first, first + GROUP)
        for j, k in enumerate(group):
            contrib = matmul(grad_rows[...], weights[k], ((1,), (1,)))
            contribs[j * VOX : (j + 1) * VOX, :] = split(contrib)
        for row in range(0, EXT, TILE):
            rows = [offset_onehot(kernel_map, k, TILE, row) for k in group]
            part = joined(matmul(jnp.concatenate(rows, axis=1), contribs[...]))
            tile = slice(row, row + TILE)
            if first > offsets[0]:
                part += ext_grad[tile, :]
            elif earlier:
                part += earlier[0][tile, :]
            ext_grad[tile, :] = part


def output_kernel(count, weights, gathered, output):
    result = matmul(weights[...].reshape(KV * C, C), gathered[...], ((0,), (0,)))
    output[...] = masked(count, result.T).astype(bf16)


def finish_kernel(count, ext_grad, for_upper, for_lower, send, grad_features):
    total = ext_grad[:VOX, :]
    for side, returned in ((1, for_upper), (0, for_lower)):
        rows = onehot(send[side : side + 1, :], VOX)
        total = total + joined(matmul(rows, split(returned[...])))
    grad_features[...] = masked(count, total).astype(bf16)


def encode(values, coded):
    top = jnp.max(jnp.abs(values), axis=0, keepdims=True)
    exponent = jnp.clip(jnp.floor(jnp.log2(jnp.maximum(top, 1e-37))), -100.0, 100.0)
    steps = jnp.round(values * jnp.exp2(14.0 - exponent))
    coded[:QUARTER, :] = jnp.clip(steps, -32767.0, 32767.0).astype(jnp.int32).astype(jnp.int16)
    exponent = jnp.broadcast_to(exponent, (CODED - QUARTER, C))
    coded[QUARTER:, :] = exponent.astype(jnp.int32).astype(jnp.int16)


def decode(coded):
    values = coded[...].astype(jnp.int32).astype(f32)
    return values[:QUARTER, :] * jnp.exp2(values[QUARTER : QUARTER + 1, :] - 14.0)


def halves_kernel(kept, received, quarters):
    for i in range(4):
        rows = slice(i * QUARTER, (i + 1) * QUARTER)
        encode(kept[rows, :] + received[rows, :], quarters.at[i])


def quarters_kernel(quarters, total):
    total[:QUARTER, :] = sum(decode(quarters.at[i]) for i in range(4))
    total[QUARTER:, :] = jnp.zeros_like(total[QUARTER:, :])


def pieces_kernel(pieces, spread):
    spread[...] = jnp.broadcast_to(jnp.sum(pieces[...], axis=0)[None], spread.shape)


def total_kernel(total, quarters):
    encode(total[:QUARTER, :], quarters.at[0])
    for i in range(1, 4):
        quarters[i] = quarters[0]


def whole_kernel(kept, received, whole, buffer, sems):
    core = lax.axis_index("c")
    copies = []
    for i, (half, place) in enumerate(((kept, core), (received, 1 - core))):
        for j in range(4):
            buffer[i, j * QUARTER : (j + 1) * QUARTER, :] = decode(half.at[j])
        rows = pl.ds(pl.multiple_of(place * HALF, 8), HALF)
        copies.append(pltpu.make_async_copy(buffer.at[i], whole.at[rows], sems.at[i]))
        copies[i].start()
    for copy in copies:
        copy.wait()


def call(kernel, name, args, outs, scratch=(), flops=0, scalars=1):
    scalar = pl.BlockSpec(memory_space=pltpu.SMEM)
    vector = pl.BlockSpec(memory_space=pltpu.VMEM)
    outs = tuple(jax.ShapeDtypeStruct(*o) for o in outs)
    moved = sum(a.size * a.dtype.itemsize for a in (*args, *outs))
    return pl.pallas_call(
        kernel,
        name=name,
        in_specs=[scalar] * scalars + [vector] * (len(args) - scalars),
        out_specs=(vector,) * len(outs),
        out_shape=outs,
        scratch_shapes=[pltpu.VMEM(*s) for s in scratch],
        cost_estimate=pl.CostEstimate(flops=flops, transcendentals=0, bytes_accessed=moved),
        compiler_params=pltpu.CompilerParams(vmem_limit_bytes=VMEM_LIMIT),
    )(*args)


def scatter(name, offsets, args):
    return call(
        functools.partial(scatter_kernel, offsets),
        name,
        args,
        [((EXT, C), f32)],
        [((GROUP * VOX, 2 * C), bf16)],
        2 * (offsets[1] - offsets[0]) * VOX * C * (C + 2 * EXT),
        scalars=0,
    )[0]


def across_c(part):
    return lax.ppermute(part, "c", [(0, 1), (1, 0)])


def exchange(pieces, axes):
    return lax.all_to_all(pieces, axes, 0, 0, tiled=False)


def per_device(features, weights, kernel_map, send_rows, counts, cotangent):
    features, kernel_map, send, cotangent = features[0], kernel_map[0], send_rows[0], cotangent[0]
    space = ("z", "y")
    size = lax.axis_size(space)
    up = [(i, i + 1) for i in range(size - 1)]
    down = [(i + 1, i) for i in range(size - 1)]
    rows = ((HALO, C), bf16)
    to_lower, to_upper = call(pick_kernel, "pick", (counts, features, send), [rows, rows])
    lower_in = lax.ppermute(to_upper, space, up)
    upper_in = lax.ppermute(to_lower, space, down)
    (own,) = call(
        local_kernel,
        "local",
        (counts, features, kernel_map),
        [((KV * C, VOX), bf16)],
        [((C, VOX), bf16)],
        2 * KV * VOX * C * VOX,
    )
    kept, sent, gathered, grad_rows = call(
        halo_kernel,
        "halo",
        (counts, lower_in, upper_in, kernel_map, own, cotangent),
        [((HALF, C), f32), ((HALF, C), f32), ((KV * C, VOX), bf16), ((VOX, C), bf16)],
        [((C, 2 * HALO), bf16)],
        2 * KV * VOX * C * (2 * HALO + C),
    )
    received = across_c(sent)
    (output,) = call(
        output_kernel,
        "output",
        (counts, weights, gathered),
        [((VOX, C), bf16)],
        flops=2 * KV * VOX * C * C,
    )
    ext_grad = scatter("scatter_first", (0, FIRST), (grad_rows, weights, kernel_map))
    received, ext_grad, output = lax.optimization_barrier((received, ext_grad, output))
    coded = ((4, CODED, C), jnp.int16)
    (quarters,) = call(halves_kernel, "halves", (kept, received), [coded], scalars=0)
    quarters = exchange(quarters, "x")
    ext_grad = scatter("scatter_rest", (FIRST, KV), (grad_rows, weights, kernel_map, ext_grad))
    for_lower = lax.ppermute(ext_grad[VOX + HALO :], space, up)
    for_upper = lax.ppermute(ext_grad[VOX : VOX + HALO], space, down)
    (grad_features,) = call(
        finish_kernel,
        "finish",
        (counts, ext_grad, for_upper, for_lower, send),
        [((VOX, C), bf16)],
    )
    quarters, grad_features = lax.optimization_barrier((quarters, grad_features))
    (total,) = call(quarters_kernel, "quarters", (quarters,), [((VOX, C), f32)], scalars=0)
    pieces = exchange(total.reshape(size, -1, C), space)
    (pieces,) = call(pieces_kernel, "pieces", (pieces,), [((size, 8, C), f32)], scalars=0)
    total = exchange(pieces, space).reshape(VOX, C)
    (quarters,) = call(total_kernel, "total", (total,), [coded], scalars=0)
    half = exchange(quarters, "x")
    grad_weights = pl.pallas_call(
        whole_kernel,
        name="whole",
        in_specs=[pl.BlockSpec(memory_space=pltpu.VMEM)] * 2,
        out_specs=pl.BlockSpec(memory_space=pl.ANY),
        out_shape=jax.ShapeDtypeStruct((KV * C, C), f32),
        scratch_shapes=[pltpu.VMEM((2, HALF, C), f32), pltpu.SemaphoreType.DMA((2,))],
        compiler_params=pltpu.CompilerParams(vmem_limit_bytes=8 * 2**20),
    )(half, across_c(half)).reshape(KV, C, C)
    return output[None], grad_features[None], grad_weights


def solution(mesh):
    fine = Mesh(mesh.devices.reshape(8, 8, 4, 2), ("z", "y", "x", "c"))
    space, batch = ("z", "y"), ("x", "c")
    in_specs = (
        P(batch, space, None),
        P(),
        P(batch, None, space),
        P(batch, None, space),
        P(batch, space),
        P(batch, space, None),
    )
    out_specs = (P(batch, space, None), P(batch, space, None), P())
    return jax.shard_map(
        per_device, mesh=fine, in_specs=in_specs, out_specs=out_specs, check_vma=False
    )
```

time: 126 us -> 111 us (0.88)
  blocking collectives: 78.2 us -> 55.3 us
  starting transfers between devices: 13.6 us -> 28.4 us
  local copies, waits for them, and re-layouts: 6.84 us -> 2.42 us
  Pallas kernels: 20.2 us -> 17.4 us
    all_to_all x5 -> x3, blocking collectives: 78.2 us -> 55.3 us  [exchange(): return lax.all_to_all(pieces, axes, 0, 0, tiled=False)]
    ppermute x2 -> x4, starting transfers between devices: 5.95 us -> 20 us  [the longest x2 14.7 us: across_c(): return lax.ppermute(part, 'c', [(0, 1), (1, 0)])]
    unnamed x14 -> x11, local copies, waits for them, and re-layouts: 5.68 us -> 2.41 us
    pallas_call x4 -> x12, Pallas kernels: 20.2 us -> 17.4 us  [the longest x11 16.1 us: call(): pl.pallas_call(kernel, name=name, in_specs=[scalar] * scalars + [vector]...]
    ppermute x2 -> x4, waiting for transfers between devices: 0.01 us -> 1.43 us  [the longest x2 1.42 us: across_c(): return lax.ppermute(part, 'c', [(0, 1), (1, 0)])]
  transfers between devices with their start and end apart: 5 -> 7, of which waited for: 2 -> 3; matrix products, arithmetic and copies ran while one was open for 1% -> 1% of each run, Pallas kernels for 11% -> 11%
where the time goes in v2:
time: 111 us; the launch traced here: 110 us
  blocking collectives  55.3 us (50%)
  starting transfers between devices  28.4 us (26%)
  Pallas kernels  17.4 us (16%)
  waiting for transfers between devices  5.14 us (5%)
  local copies, waits for them, and re-layouts  2.42 us (2%)
  between operations  1.62 us (1%)
    all_to_all x3, blocking collectives, exchange(): return lax.all_to_all(pieces, axes, 0, 0, tiled=False)  55.3 us
    pallas_call x11, Pallas kernels, call(): pl.pallas_call(kernel, name=name, in_specs=[scalar] * scalars + [vector]...  16.1 us
    ppermute x2, starting transfers between devices, across_c(): return lax.ppermute(part, 'c', [(0, 1), (1, 0)])  14.7 us
    ppermute x1, starting transfers between devices, per_device(): lower_in = lax.ppermute(to_upper, space, up)  4.03 us
    all_to_all x1, starting transfers between devices, exchange(): return lax.all_to_all(pieces, axes, 0, 0, tiled=False)  3.65 us
    ppermute x1, waiting for transfers between devices, per_device(): for_upper = lax.ppermute(ext_grad[VOX:VOX + HALO], space, down)  3.52 us
    ppermute x1, starting transfers between devices, per_device(): for_lower = lax.ppermute(ext_grad[VOX + HALO:], space, up)  3.47 us
    unnamed x11, local copies, waits for them, and re-layouts  2.41 us
  transfers between devices with their start and end apart: 7, of which 3 were waited for; matrix products, arithmetic and copies ran while one was open for 1% of the time, Pallas kernels for 11%

profile of v2, /device:TPU:1, one launch (start us, length us, event | category | flops | bytes accessed | tf_op | source)
XLA Modules:
  0.0 110.3 jit_solution(13242264931269669824)
XLA Ops:
  1.3 0.9 copy-done.1
  2.2 0.7 copy-done.2
  2.9 0.3 pick.1
  3.2 4.0 %collective-permute-start = (bf16[128,128]{1,0:T(8,128)(2,1)S(1)}, bf16[128,128]{1,0:T(8,128)(2,1)S(1)}, u32[]{:S(2)}, u32[]{:S(2)}) collective-permute-start(bf16[128,128]{1,0:T(8,128)(2,1)S(1)} %get-tuple-element.14), channel_id=1, source_target_pairs={{0,8},{8,16},{16,24},{24,32},{32,40},{40,48},{48,56},{56,64},{64,7... | collective-permute-start | bytes 98312 | tf_op jit(solution)/shard_map/ppermute | solution.py:212
  7.2 1.3 %collective-permute-start.1 = (bf16[128,128]{1,0:T(8,128)(2,1)S(1)}, bf16[128,128]{1,0:T(8,128)(2,1)S(1)}, u32[]{:S(2)}, u32[]{:S(2)}) collective-permute-start(bf16[128,128]{1,0:T(8,128)(2,1)S(1)} %get-tuple-element.15), channel_id=1, source_target_pairs={{8,0},{16,8},{24,16},{32,24},{40,32},{48,40},{56,48},{64,56},{72,6... | collective-permute-start | bytes 98312 | tf_op jit(solution)/shard_map/ppermute | solution.py:213
  8.5 0.8 copy.11
  9.3 2.8 %local.1.own = bf16[3456,512]{1,0:T(8,128)(2,1)S(1)} custom-call(s32[1,1]{1,0:T(1,128)S(6)} %copy.12.count, bf16[512,128]{1,0:T(8,128)(2,1)S(1)} %bitcast.14, s32[27,512]{1,0:T(8,128)S(1)} %bitcast.15), custom_call_target="tpu_custom_call" | custom-call | flops 1811939328 | bytes 3725316 | tf_op jit(solution)/shard_map/local/pallas_call | solution.py:172
  12.2 0.0 copy-start
  12.2 0.0 collective-permute-done.lower
  12.2 0.0 collective-permute-done.1.upper
  12.2 2.2 %halo.1 = (f32[1728,128]{1,0:T(8,128)S(1)}, f32[1728,128]{1,0:T(8,128)S(1)}, bf16[3456,512]{1,0:T(8,128)(2,1)S(1)}, bf16[512,128]{1,0:T(8,128)(2,1)S(1)}) custom-call(s32[1,1]{1,0:T(1,128)S(6)} %copy.12.count, bf16[128,128]{1,0:T(8,128)(2,1)S(1)} %collective-permute-done.lower, bf16[128,128]{1,0:T(8,128)(2,1)S(1)} %collective-permute-done.1.upper, ...), custom_call_target="tpu_custom_call" | custom-call | flops 1358954496 | bytes 9230340 | tf_op jit(solution)/shard_map/halo/pallas_call | solution.py:172
  14.4 6.8 %collective-permute-start.2 = (f32[1728,128]{1,0:T(8,128)S(1)}, f32[1728,128]{1,0:T(8,128)S(1)}, u32[]{:S(2)}, u32[]{:S(2)}) collective-permute-start(f32[1728,128]{1,0:T(8,128)S(1)} %get-tuple-element.16), channel_id=1, source_target_pairs={{0,1},{1,0},{2,3},{3,2},{4,5},{5,4},{6,7},{7,6},{8,9},{9,8},{10,11... | collective-permute-start | bytes 2654216 | tf_op jit(solution)/shard_map/ppermute | solution.py:197
  21.3 1.4 %output.1 = bf16[512,128]{1,0:T(8,128)(2,1)} custom-call(s32[1,1]{1,0:T(1,128)S(6)} %copy.12.count, bf16[27,128,128]{2,1,0:T(8,128)(2,1)S(1)} %copy-done, bf16[3456,512]{1,0:T(8,128)(2,1)S(1)} %get-tuple-element.18.gathered), custom_call_target="tpu_custom_call" | custom-call | flops 452984832 | bytes 4554756 | tf_op jit(solution)/shard_map/output/pallas_call | solution.py:172
  22.7 1.7 %scatter_first.1.refs_0_ = f32[768,128]{1,0:T(8,128)S(1)} custom-call(bf16[512,128]{1,0:T(8,128)(2,1)S(1)} %get-tuple-element.17.grad_rows, bf16[27,128,128]{2,1,0:T(8,128)(2,1)S(1)} %copy-done, s32[27,512]{1,0:T(8,128)S(1)} %bitcast.17), custom_call_target="tpu_custom_call" | custom-call | flops 1308622848 | bytes 1464320 | tf_op jit(solution)/shard_map/scatter_first/pallas_call | solution.py:172
  24.4 1.0 halves.1
  25.5 3.6 %all-to-all-start = ((s16[4,448,128]{2,1,0:T(8,128)(2,1)}), s16[4,448,128]{2,1,0:T(8,128)(2,1)S(1)}, u32[]{:S(2)}, u32[]{:S(2)}) async-start(s16[4,448,128]{2,1,0:T(8,128)(2,1)} %halves.1), calls=%async_computation | async-start | bytes 917504 | tf_op jit(solution)/shard_map/all_to_all | solution.py:201
  29.1 0.0 copy-start.3
  29.1 5.4 %scatter_rest.1.ext_grad = f32[768,128]{1,0:T(8,128)S(1)} custom-call(bf16[512,128]{1,0:T(8,128)(2,1)S(1)} %get-tuple-element.17.grad_rows, bf16[27,128,128]{2,1,0:T(8,128)(2,1)S(1)} %copy-done, s32[27,512]{1,0:T(8,128)S(1)} %bitcast.18, f32[768,128]{1,0:T(8,128)S(1)} %scatter_first.1.refs_0_), custom_call_target="tpu_custom_call" | custom-call | flops 4580179968 | bytes 1857536 | tf_op jit(solution)/shard_map/scatter_rest/pallas_call | solution.py:172
  34.5 3.5 %collective-permute-start.4 = (f32[128,128]{1,0:T(8,128)S(1)}, f32[128,128]{1,0:T(8,128)S(1)}, u32[]{:S(2)}, u32[]{:S(2)}) collective-permute-start(f32[128,128]{1,0:T(8,128)S(1)} %get-tuple-element.25), channel_id=1, source_target_pairs={{0,8},{8,16},{16,24},{24,32},{32,40},{40,48},{48,56},{56,64},{64,7... | collective-permute-start | bytes 196616 | tf_op jit(solution)/shard_map/ppermute | solution.py:244
  38.0 1.3 %collective-permute-start.3 = (f32[128,128]{1,0:T(8,128)S(1)}, f32[128,128]{1,0:T(8,128)S(1)}, u32[]{:S(2)}, u32[]{:S(2)}) collective-permute-start(f32[128,128]{1,0:T(8,128)S(1)} %get-tuple-element.26), channel_id=1, source_target_pairs={{8,0},{16,8},{24,16},{32,24},{40,32},{48,40},{56,48},{64,56},{72,6... | collective-permute-start | bytes 196616 | tf_op jit(solution)/shard_map/ppermute | solution.py:245
  39.3 0.2 collective-permute-done.4.for_lower
  39.5 3.5 %collective-permute-done.3.for_upper = f32[128,128]{1,0:T(8,128)S(1)} collective-permute-done((f32[128,128]{1,0:T(8,128)S(1)}, f32[128,128]{1,0:T(8,128)S(1)}, u32[]{:S(2)}, u32[]{:S(2)}) %collective-permute-start.3) | collective-permute-done | bytes 65568 | tf_op jit(solution)/shard_map/ppermute | solution.py:245
  43.0 0.9 finish.1
  44.0 0.1 quarters.1
  44.1 28.3 %all_to_all.20.pieces = f32[64,8,128]{2,1,0:T(8,128)S(1)} all-to-all(f32[64,8,128]{2,1,0:T(8,128)S(1)} %bitcast.11), channel_id=1, replica_groups=mesh['z'=8,'y'=8,'x'=4,'c'=2] {'z','y'}, dimensions={0} | all-to-all | bytes 524288 | tf_op jit(solution)/shard_map/all_to_all | solution.py:201
  72.4 0.1 pieces.1
  72.5 17.4 %all_to_all.21 = f32[64,8,128]{2,1,0:T(8,128)S(1)} all-to-all(f32[64,8,128]{2,1,0:T(8,128)S(1)} %pieces.1), channel_id=1, replica_groups=mesh['z'=8,'y'=8,'x'=4,'c'=2] {'z','y'}, dimensions={0} | all-to-all | bytes 524288 | tf_op jit(solution)/shard_map/all_to_all | solution.py:201
  89.9 0.1 total.1
  90.0 9.5 %all_to_all.22.kept = s16[4,448,128]{2,1,0:T(8,128)(2,1)S(1)} all-to-all(s16[4,448,128]{2,1,0:T(8,128)(2,1)S(1)} %total.1), channel_id=1, replica_groups=mesh['z'=8,'y'=8,'x'=4,'c'=2] {'x'}, dimensions={0} | all-to-all | bytes 917504 | tf_op jit(solution)/shard_map/all_to_all | solution.py:201
  99.5 7.8 %collective-permute-start.5 = (s16[4,448,128]{2,1,0:T(8,128)(2,1)S(1)}, s16[4,448,128]{2,1,0:T(8,128)(2,1)S(1)}, u32[]{:S(2)}, u32[]{:S(2)}) collective-permute-start(s16[4,448,128]{2,1,0:T(8,128)(2,1)S(1)} %all_to_all.22.kept), channel_id=1, source_target_pairs={{0,1},{1,0},{2,3},{3,2},{4,5},{5,4},{6,7},{7,6},{8,9},{9,8},{10,11... | collective-permute-start | bytes 1376264 | tf_op jit(solution)/shard_map/ppermute | solution.py:197
  107.4 1.4 %collective-permute-done.5.received = s16[4,448,128]{2,1,0:T(8,128)(2,1)S(1)} collective-permute-done((s16[4,448,128]{2,1,0:T(8,128)(2,1)S(1)}, s16[4,448,128]{2,1,0:T(8,128)(2,1)S(1)}, u32[]{:S(2)}, u32[]{:S(2)}) %collective-permute-start.5) | collective-permute-done | bytes 458784 | tf_op jit(solution)/shard_map/ppermute | solution.py:197
  108.8 1.3 %whole.1 = f32[3456,128]{1,0:T(8,128)} custom-call(s16[4,448,128]{2,1,0:T(8,128)(2,1)S(1)} %all_to_all.22.kept, s16[4,448,128]{2,1,0:T(8,128)(2,1)S(1)} %collective-permute-done.5.received), custom_call_target="tpu_custom_call" | custom-call | tf_op jit(solution)/shard_map/whole/pallas_call | solution.py:259
  (9 shorter events, 0.0 us)
Async XLA Ops:
  1.3 0.9 copy-start.1
  2.2 0.7 copy-start.2
  2.9 9.4 %copy-start.4 = (bf16[1,512,128]{2,1,0:T(8,128)(2,1)S(1)}, bf16[1,512,128]{2,1,0:T(8,128)(2,1)}, u32[]{:S(2)}) copy-start(bf16[1,512,128]{2,1,0:T(8,128)(2,1)} %param.11) | copy-start | bytes 393220
  3.2 9.0 %collective-permute-start = (bf16[128,128]{1,0:T(8,128)(2,1)S(1)}, bf16[128,128]{1,0:T(8,128)(2,1)S(1)}, u32[]{:S(2)}, u32[]{:S(2)}) collective-permute-start(bf16[128,128]{1,0:T(8,128)(2,1)S(1)} %get-tuple-element.14), channel_id=1, source_target_pairs={{0,8},{8,16},{16,24},{24,32},{32,40},{40,48},{48,56},{56,64},{64,7... | collective-permute-start | bytes 98312 | tf_op jit(solution)/shard_map/ppermute | solution.py:212
  7.2 5.0 %collective-permute-start.1 = (bf16[128,128]{1,0:T(8,128)(2,1)S(1)}, bf16[128,128]{1,0:T(8,128)(2,1)S(1)}, u32[]{:S(2)}, u32[]{:S(2)}) collective-permute-start(bf16[128,128]{1,0:T(8,128)(2,1)S(1)} %get-tuple-element.15), channel_id=1, source_target_pairs={{8,0},{16,8},{24,16},{32,24},{40,32},{48,40},{56,48},{64,56},{72,6... | collective-permute-start | bytes 98312 | tf_op jit(solution)/shard_map/ppermute | solution.py:213
  12.2 9.1 %copy-start = (bf16[27,128,128]{2,1,0:T(8,128)(2,1)S(1)}, bf16[27,128,128]{2,1,0:T(8,128)(2,1)}, u32[]{:S(2)}) copy-start(bf16[27,128,128]{2,1,0:T(8,128)(2,1)} %weights.5) | copy-start | bytes 2654212
  14.4 10.0 %collective-permute-start.2 = (f32[1728,128]{1,0:T(8,128)S(1)}, f32[1728,128]{1,0:T(8,128)S(1)}, u32[]{:S(2)}, u32[]{:S(2)}) collective-permute-start(f32[1728,128]{1,0:T(8,128)S(1)} %get-tuple-element.16), channel_id=1, source_target_pairs={{0,1},{1,0},{2,3},{3,2},{4,5},{5,4},{6,7},{7,6},{8,9},{9,8},{10,11... | collective-permute-start | bytes 2654216 | tf_op jit(solution)/shard_map/ppermute | solution.py:197
  25.5 18.5 %all-to-all-start = ((s16[4,448,128]{2,1,0:T(8,128)(2,1)}), s16[4,448,128]{2,1,0:T(8,128)(2,1)S(1)}, u32[]{:S(2)}, u32[]{:S(2)}) async-start(s16[4,448,128]{2,1,0:T(8,128)(2,1)} %halves.1), calls=%async_computation | async-start | bytes 917504 | tf_op jit(solution)/shard_map/all_to_all | solution.py:201
  29.1 13.9 %copy-start.3 = (s32[1,2,128]{2,1,0:T(2,128)S(1)}, s32[1,2,128]{2,1,0:T(2,128)}, u32[]{:S(2)}) copy-start(s32[1,2,128]{2,1,0:T(2,128)} %param.9) | copy-start | bytes 3076
  34.5 5.0 %collective-permute-start.4 = (f32[128,128]{1,0:T(8,128)S(1)}, f32[128,128]{1,0:T(8,128)S(1)}, u32[]{:S(2)}, u32[]{:S(2)}) collective-permute-start(f32[128,128]{1,0:T(8,128)S(1)} %get-tuple-element.25), channel_id=1, source_target_pairs={{0,8},{8,16},{16,24},{24,32},{32,40},{40,48},{48,56},{56,64},{64,7... | collective-permute-start | bytes 196616 | tf_op jit(solution)/shard_map/ppermute | solution.py:244
  38.0 5.0 %collective-permute-start.3 = (f32[128,128]{1,0:T(8,128)S(1)}, f32[128,128]{1,0:T(8,128)S(1)}, u32[]{:S(2)}, u32[]{:S(2)}) collective-permute-start(f32[128,128]{1,0:T(8,128)S(1)} %get-tuple-element.26), channel_id=1, source_target_pairs={{8,0},{16,8},{24,16},{32,24},{40,32},{48,40},{56,48},{64,56},{72,6... | collective-permute-start | bytes 196616 | tf_op jit(solution)/shard_map/ppermute | solution.py:245
  99.5 9.3 %collective-permute-start.5 = (s16[4,448,128]{2,1,0:T(8,128)(2,1)S(1)}, s16[4,448,128]{2,1,0:T(8,128)(2,1)S(1)}, u32[]{:S(2)}, u32[]{:S(2)}) collective-permute-start(s16[4,448,128]{2,1,0:T(8,128)(2,1)S(1)} %all_to_all.22.kept), channel_id=1, source_target_pairs={{0,1},{1,0},{2,3},{3,2},{4,5},{5,4},{6,7},{7,6},{8,9},{9,8},{10,11... | collective-permute-start | bytes 1376264 | tf_op jit(solution)/shard_map/ppermute | solution.py:197

commit v3 on v2

--- a/solution.py
+++ b/solution.py
@@ -17,7 +17,7 @@
 QUARTER = HALF // 4
 CODED = QUARTER + 16
 GROUP = 3
-FIRST = 6
+FIRST = 3
 TILE = 256
 VMEM_LIMIT = 16 * 2**20
 
@@ -31,7 +31,7 @@
 
 
 def offset_onehot(kernel_map, k, rows, first=0):
-    return onehot(kernel_map[k : k + 1, :], rows, first)
+    return onehot(kernel_map[k], rows, first)
 
 
 def masked(count, values):
@@ -53,15 +53,27 @@
     return lax.dot_general(a, b, (dims, ((), ())), preferred_element_type=f32)
 
 
-def pick_kernel(count, features, send, to_lower, to_upper):
-    live = masked(count, features[...])
+def pick_kernel(
+    count, features, send, kernel_map, to_lower, to_upper, table, kernel_map_out, rows, lists, sems
+):
+    copies = [
+        pltpu.make_async_copy(source, target, sems.at[i])
+        for i, (source, target) in enumerate(
+            ((features, rows), (send, lists), (kernel_map, kernel_map_out))
+        )
+    ]
+    for copy in copies:
+        copy.start()
+    for copy in copies:
+        copy.wait()
+    live = masked(count, rows[...])
     for side, outgoing in ((0, to_lower), (1, to_upper)):
-        rows = onehot(send[side : side + 1, :], VOX)
-        outgoing[...] = matmul(rows, live, ((0,), (0,))).astype(bf16)
-
-
-def local_kernel(count, features, kernel_map, gathered, table):
-    table[...] = masked(count, features[...]).T
+        picked = onehot(lists[side : side + 1, :], VOX)
+        outgoing[...] = matmul(picked, live, ((0,), (0,))).astype(bf16)
+    table[...] = live.T
+
+
+def local_kernel(table, kernel_map, gathered):
     for k in range(KV):
         rows = offset_onehot(kernel_map, k, VOX)
         gathered[k * C : (k + 1) * C, :] = matmul(table[...], rows).astype(bf16)
@@ -164,18 +176,19 @@
         copy.wait()
 
 
-def call(kernel, name, args, outs, scratch=(), flops=0, scalars=1):
+def call(kernel, name, args, outs, scratch=(), flops=0, scalars=1, space=pltpu.VMEM):
     scalar = pl.BlockSpec(memory_space=pltpu.SMEM)
     vector = pl.BlockSpec(memory_space=pltpu.VMEM)
+    operand = pl.BlockSpec(memory_space=space)
     outs = tuple(jax.ShapeDtypeStruct(*o) for o in outs)
     moved = sum(a.size * a.dtype.itemsize for a in (*args, *outs))
     return pl.pallas_call(
         kernel,
         name=name,
-        in_specs=[scalar] * scalars + [vector] * (len(args) - scalars),
+        in_specs=[scalar] * scalars + [operand] * (len(args) - scalars),
         out_specs=(vector,) * len(outs),
         out_shape=outs,
-        scratch_shapes=[pltpu.VMEM(*s) for s in scratch],
+        scratch_shapes=[pltpu.VMEM(*s) if isinstance(s, tuple) else s for s in scratch],
         cost_estimate=pl.CostEstimate(flops=flops, transcendentals=0, bytes_accessed=moved),
         compiler_params=pltpu.CompilerParams(vmem_limit_bytes=VMEM_LIMIT),
     )(*args)
@@ -202,22 +215,30 @@
 
 
 def per_device(features, weights, kernel_map, send_rows, counts, cotangent):
-    features, kernel_map, send, cotangent = features[0], kernel_map[0], send_rows[0], cotangent[0]
+    features, send, cotangent = features[0], send_rows[0], cotangent[0]
+    kernel_map = kernel_map.transpose(1, 0, 2)
     space = ("z", "y")
     size = lax.axis_size(space)
     up = [(i, i + 1) for i in range(size - 1)]
     down = [(i + 1, i) for i in range(size - 1)]
     rows = ((HALO, C), bf16)
-    to_lower, to_upper = call(pick_kernel, "pick", (counts, features, send), [rows, rows])
+    to_lower, to_upper, table, kernel_map = call(
+        pick_kernel,
+        "pick",
+        (counts, *(pltpu.with_memory_space_constraint(a, pltpu.HBM) for a in (features, send, kernel_map))),
+        [rows, rows, ((C, VOX), bf16), ((KV, 1, VOX), jnp.int32)],
+        [((VOX, C), bf16), ((2, HALO), jnp.int32), pltpu.SemaphoreType.DMA((3,))],
+        space=pltpu.HBM,
+    )
     lower_in = lax.ppermute(to_upper, space, up)
     upper_in = lax.ppermute(to_lower, space, down)
     (own,) = call(
         local_kernel,
         "local",
-        (counts, features, kernel_map),
+        (table, kernel_map),
         [((KV * C, VOX), bf16)],
-        [((C, VOX), bf16)],
-        2 * KV * VOX * C * VOX,
+        flops=2 * KV * VOX * C * VOX,
+        scalars=0,
     )
     kept, sent, gathered, grad_rows = call(
         halo_kernel,
@@ -241,21 +262,25 @@
     (quarters,) = call(halves_kernel, "halves", (kept, received), [coded], scalars=0)
     quarters = exchange(quarters, "x")
     ext_grad = scatter("scatter_rest", (FIRST, KV), (grad_rows, weights, kernel_map, ext_grad))
+    quarters, ext_grad = lax.optimization_barrier((quarters, ext_grad))
+    (total,) = call(quarters_kernel, "quarters", (quarters,), [((VOX, C), f32)], scalars=0)
+    pieces = exchange(total.reshape(size, -1, C), space)
     for_lower = lax.ppermute(ext_grad[VOX + HALO :], space, up)
     for_upper = lax.ppermute(ext_grad[VOX : VOX + HALO], space, down)
+    pieces, for_lower, for_upper = lax.optimization_barrier((pieces, for_lower, for_upper))
+    (pieces,) = call(pieces_kernel, "pieces", (pieces,), [((size, 8, C), f32)], scalars=0)
+    total = exchange(pieces, space).reshape(VOX, C)
+    (quarters,) = call(total_kernel, "total", (total,), [coded], scalars=0)
+    half = exchange(quarters, "x")
+    half, ext_grad = lax.optimization_barrier((half, ext_grad))
+    received = across_c(half)
     (grad_features,) = call(
         finish_kernel,
         "finish",
         (counts, ext_grad, for_upper, for_lower, send),
         [((VOX, C), bf16)],
     )
-    quarters, grad_features = lax.optimization_barrier((quarters, grad_features))
-    (total,) = call(quarters_kernel, "quarters", (quarters,), [((VOX, C), f32)], scalars=0)
-    pieces = exchange(total.reshape(size, -1, C), space)
-    (pieces,) = call(pieces_kernel, "pieces", (pieces,), [((size, 8, C), f32)], scalars=0)
-    total = exchange(pieces, space).reshape(VOX, C)
-    (quarters,) = call(total_kernel, "total", (total,), [coded], scalars=0)
-    half = exchange(quarters, "x")
+    received, grad_features = lax.optimization_barrier((received, grad_features))
     grad_weights = pl.pallas_call(
         whole_kernel,
         name="whole",
@@ -264,7 +289,7 @@
         out_shape=jax.ShapeDtypeStruct((KV * C, C), f32),
         scratch_shapes=[pltpu.VMEM((2, HALF, C), f32), pltpu.SemaphoreType.DMA((2,))],
         compiler_params=pltpu.CompilerParams(vmem_limit_bytes=8 * 2**20),
-    )(half, across_c(half)).reshape(KV, C, C)
+    )(half, received).reshape(KV, C, C)
     return output[None], grad_features[None], grad_weights
 
 

time: 111 us -> 104 us (0.937)
  blocking collectives: 55.3 us -> 29.4 us
  starting transfers between devices: 28.4 us -> 42.5 us
  waiting for transfers between devices: 5.14 us -> 11.5 us
  local copies, waits for them, and re-layouts: 2.42 us -> 0.03 us
    all_to_all x3 -> x2, blocking collectives: 55.3 us -> 29.4 us  [exchange(): return lax.all_to_all(pieces, axes, 0, 0, tiled=False)]
    all_to_all x1 -> x2, starting transfers between devices: 3.65 us -> 17.2 us  [exchange(): return lax.all_to_all(pieces, axes, 0, 0, tiled=False)]
    all_to_all x1 -> x2, waiting for transfers between devices: 0.01 us -> 8.03 us  [exchange(): return lax.all_to_all(pieces, axes, 0, 0, tiled=False)]
    unnamed x11 -> x6, local copies, waits for them, and re-layouts: 2.41 us -> 0.02 us
    ppermute x1, waiting for transfers between devices: 3.52 us -> 1.87 us  [per_device(): for_upper = lax.ppermute(ext_grad[VOX:VOX + HALO], space, down)]
    ppermute x1, waiting for transfers between devices: 0.01 us -> 1.13 us  [per_device(): upper_in = lax.ppermute(to_lower, space, down)]
  transfers between devices with their start and end apart: 7 -> 8, of which waited for: 3 -> 5; matrix products, arithmetic and copies ran while one was open for 1% -> 0% of each run, Pallas kernels for 11% -> 11%
where the time goes in v3:
time: 104 us; the launch traced here: 103 us
  starting transfers between devices  42.5 us (41%)
  blocking collectives  29.4 us (28%)
  Pallas kernels  18.4 us (18%)
  waiting for transfers between devices  11.5 us (11%)
  between operations  1.66 us (2%)
    all_to_all x2, blocking collectives, exchange(): return lax.all_to_all(pieces, axes, 0, 0, tiled=False)  29.4 us
    all_to_all x2, starting transfers between devices, exchange(): return lax.all_to_all(pieces, axes, 0, 0, tiled=False)  17.2 us
    pallas_call x11, Pallas kernels, call(): pl.pallas_call(kernel, name=name, in_specs=[scalar] * scalars + [operand]...  17 us
    ppermute x2, starting transfers between devices, across_c(): return lax.ppermute(part, 'c', [(0, 1), (1, 0)])  14.7 us
    all_to_all x2, waiting for transfers between devices, exchange(): return lax.all_to_all(pieces, axes, 0, 0, tiled=False)  8.03 us
    ppermute x1, starting transfers between devices, per_device(): lower_in = lax.ppermute(to_upper, space, up)  4.03 us
    ppermute x1, starting transfers between devices, per_device(): for_lower = lax.ppermute(ext_grad[VOX + HALO:], space, up)  3.99 us
  transfers between devices with their start and end apart: 8, of which 5 were waited for; matrix products, arithmetic and copies ran while one was open for 0% of the time, Pallas kernels for 11%

profile of v3, /device:TPU:1, one launch (start us, length us, event | category | flops | bytes accessed | tf_op | source)
XLA Modules:
  0.0 103.4 jit_solution(5968537296891072310)
XLA Ops:
  1.3 1.2 %pick.1 = (bf16[128,128]{1,0:T(8,128)(2,1)S(1)}, bf16[128,128]{1,0:T(8,128)(2,1)S(1)}, bf16[128,512]{1,0:T(8,128)(2,1)S(1)}, s32[27,1,512]{2,1,0:T(1,128)S(1)}) custom-call(s32[1,1]{1,0:T(1,128)S(6)} %copy.9.count, bf16[512,128]{1,0:T(8,128)(2,1)} %bitcast.15, s32[2,128]{1,0:T(2,128)} %bitcast.10, s32[27,1,512]{2,1,0:T(1,128)} %bitcast.17), custom_call_target="tpu_custom_call" | custom-call | bytes 439300 | tf_op jit(solution)/shard_map/pick/pallas_call | solution.py:185
  2.6 4.0 %collective-permute-start = (bf16[128,128]{1,0:T(8,128)(2,1)S(1)}, bf16[128,128]{1,0:T(8,128)(2,1)S(1)}, u32[]{:S(2)}, u32[]{:S(2)}) collective-permute-start(bf16[128,128]{1,0:T(8,128)(2,1)S(1)} %get-tuple-element.23), channel_id=1, source_target_pairs={{0,8},{8,16},{16,24},{24,32},{32,40},{40,48},{48,56},{56,64},{64,7... | collective-permute-start | bytes 98312 | tf_op jit(solution)/shard_map/ppermute | solution.py:233
  6.6 1.3 %collective-permute-start.1 = (bf16[128,128]{1,0:T(8,128)(2,1)S(1)}, bf16[128,128]{1,0:T(8,128)(2,1)S(1)}, u32[]{:S(2)}, u32[]{:S(2)}) collective-permute-start(bf16[128,128]{1,0:T(8,128)(2,1)S(1)} %get-tuple-element.24), channel_id=1, source_target_pairs={{8,0},{16,8},{24,16},{32,24},{40,32},{48,40},{56,48},{64,56},{72,6... | collective-permute-start | bytes 98312 | tf_op jit(solution)/shard_map/ppermute | solution.py:234
  7.9 2.2 %local.1.own = bf16[3456,512]{1,0:T(8,128)(2,1)S(1)} custom-call(bf16[128,512]{1,0:T(8,128)(2,1)S(1)} %get-tuple-element.26.table, s32[27,1,512]{2,1,0:T(1,128)S(1)} %get-tuple-element.25.kernel_map), custom_call_target="tpu_custom_call" | custom-call | flops 1811939328 | bytes 3725312 | tf_op jit(solution)/shard_map/local/pallas_call | solution.py:185
  10.1 0.0 copy-start
  10.1 0.0 collective-permute-done.lower
  10.1 1.1 %collective-permute-done.1.upper = bf16[128,128]{1,0:T(8,128)(2,1)S(1)} collective-permute-done((bf16[128,128]{1,0:T(8,128)(2,1)S(1)}, bf16[128,128]{1,0:T(8,128)(2,1)S(1)}, u32[]{:S(2)}, u32[]{:S(2)}) %collective-permute-start.1) | collective-permute-done | bytes 32800 | tf_op jit(solution)/shard_map/ppermute | solution.py:234
  11.3 2.1 %halo.1 = (f32[1728,128]{1,0:T(8,128)S(1)}, f32[1728,128]{1,0:T(8,128)S(1)}, bf16[3456,512]{1,0:T(8,128)(2,1)S(1)}, bf16[512,128]{1,0:T(8,128)(2,1)S(1)}) custom-call(s32[1,1]{1,0:T(1,128)S(6)} %copy.9.count, bf16[128,128]{1,0:T(8,128)(2,1)S(1)} %collective-permute-done.lower, bf16[128,128]{1,0:T(8,128)(2,1)S(1)} %collective-permute-done.1.upper, ...), custom_call_target="tpu_custom_call" | custom-call | flops 1358954496 | bytes 9230340 | tf_op jit(solution)/shard_map/halo/pallas_call | solution.py:185
  13.4 7.2 %collective-permute-start.2 = (f32[1728,128]{1,0:T(8,128)S(1)}, f32[1728,128]{1,0:T(8,128)S(1)}, u32[]{:S(2)}, u32[]{:S(2)}) collective-permute-start(f32[1728,128]{1,0:T(8,128)S(1)} %get-tuple-element.27), channel_id=1, source_target_pairs={{0,1},{1,0},{2,3},{3,2},{4,5},{5,4},{6,7},{7,6},{8,9},{9,8},{10,11... | collective-permute-start | bytes 2654216 | tf_op jit(solution)/shard_map/ppermute | solution.py:210
  20.6 1.4 %output.1 = bf16[512,128]{1,0:T(8,128)(2,1)} custom-call(s32[1,1]{1,0:T(1,128)S(6)} %copy.9.count, bf16[27,128,128]{2,1,0:T(8,128)(2,1)S(1)} %copy-done, bf16[3456,512]{1,0:T(8,128)(2,1)S(1)} %get-tuple-element.29.gathered), custom_call_target="tpu_custom_call" | custom-call | flops 452984832 | bytes 4554756 | tf_op jit(solution)/shard_map/output/pallas_call | solution.py:185
  22.0 1.0 %scatter_first.1.refs_0_ = f32[768,128]{1,0:T(8,128)S(1)} custom-call(bf16[512,128]{1,0:T(8,128)(2,1)S(1)} %get-tuple-element.28.grad_rows, bf16[27,128,128]{2,1,0:T(8,128)(2,1)S(1)} %copy-done, s32[27,1,512]{2,1,0:T(1,128)S(1)} %get-tuple-element.25.kernel_map), custom_call_target="tpu_custom_call" | custom-call | flops 654311424 | bytes 1464320 | tf_op jit(solution)/shard_map/scatter_first/pallas_call | solution.py:185
  23.1 0.0 collective-permute-done.2.received
  23.1 1.0 halves.1
  24.1 3.6 %all-to-all-start = ((s16[4,448,128]{2,1,0:T(8,128)(2,1)}), s16[4,448,128]{2,1,0:T(8,128)(2,1)S(1)}, u32[]{:S(2)}, u32[]{:S(2)}) async-start(s16[4,448,128]{2,1,0:T(8,128)(2,1)} %halves.1), calls=%async_computation | async-start | bytes 917504 | tf_op jit(solution)/shard_map/all_to_all | solution.py:214
  27.8 6.0 %scatter_rest.1.ext_grad = f32[768,128]{1,0:T(8,128)S(1)} custom-call(bf16[512,128]{1,0:T(8,128)(2,1)S(1)} %get-tuple-element.28.grad_rows, bf16[27,128,128]{2,1,0:T(8,128)(2,1)S(1)} %copy-done, s32[27,1,512]{2,1,0:T(1,128)S(1)} %get-tuple-element.25.kernel_map, f32[768,128]{1,0:T(8,128)S(1)} %scatter_first.1.refs_0_), custom_call_target="tpu_custom_call" | custom-call | flops 5234491392 | bytes 1857536 | tf_op jit(solution)/shard_map/scatter_rest/pallas_call | solution.py:185
  33.8 0.0 copy-start.1
  33.8 2.7 %all-to-all-done.quarters = s16[4,448,128]{2,1,0:T(8,128)(2,1)S(1)} async-done(((s16[4,448,128]{2,1,0:T(8,128)(2,1)}), s16[4,448,128]{2,1,0:T(8,128)(2,1)S(1)}, u32[]{:S(2)}, u32[]{:S(2)}) %all-to-all-start) | async-done | bytes 458784 | tf_op jit(solution)/shard_map/all_to_all | solution.py:214
  36.5 0.8 quarters.1
  37.3 13.6 %all-to-all-start.1 = ((f32[64,8,128]{2,1,0:T(8,128)}), f32[64,8,128]{2,1,0:T(8,128)S(1)}, u32[]{:S(2)}, u32[]{:S(2)}) async-start(f32[64,8,128]{2,1,0:T(8,128)} %bitcast.5), calls=%async_computation.1 | async-start | bytes 524288 | tf_op jit(solution)/shard_map/all_to_all | solution.py:214
  50.9 1.3 %collective-permute-start.4 = (f32[128,128]{1,0:T(8,128)S(1)}, f32[128,128]{1,0:T(8,128)S(1)}, u32[]{:S(2)}, u32[]{:S(2)}) collective-permute-start(f32[128,128]{1,0:T(8,128)S(1)} %get-tuple-element.43), channel_id=1, source_target_pairs={{8,0},{16,8},{24,16},{32,24},{40,32},{48,40},{56,48},{64,56},{72,6... | collective-permute-start | bytes 196616 | tf_op jit(solution)/shard_map/ppermute | solution.py:269
  52.2 4.0 %collective-permute-start.3 = (f32[128,128]{1,0:T(8,128)S(1)}, f32[128,128]{1,0:T(8,128)S(1)}, u32[]{:S(2)}, u32[]{:S(2)}) collective-permute-start(f32[128,128]{1,0:T(8,128)S(1)} %get-tuple-element.44), channel_id=1, source_target_pairs={{0,8},{8,16},{16,24},{24,32},{32,40},{40,48},{48,56},{56,64},{64,7... | collective-permute-start | bytes 196616 | tf_op jit(solution)/shard_map/ppermute | solution.py:268
  56.2 1.9 %collective-permute-done.4.for_upper = f32[128,128]{1,0:T(8,128)S(1)} collective-permute-done((f32[128,128]{1,0:T(8,128)S(1)}, f32[128,128]{1,0:T(8,128)S(1)}, u32[]{:S(2)}, u32[]{:S(2)}) %collective-permute-start.4) | collective-permute-done | bytes 65568 | tf_op jit(solution)/shard_map/ppermute | solution.py:269
  58.1 0.0 collective-permute-done.3.for_lower
  58.1 5.4 %all-to-all-done.1.pieces = f32[64,8,128]{2,1,0:T(8,128)S(1)} async-done(((f32[64,8,128]{2,1,0:T(8,128)}), f32[64,8,128]{2,1,0:T(8,128)S(1)}, u32[]{:S(2)}, u32[]{:S(2)}) %all-to-all-start.1) | async-done | bytes 262176 | tf_op jit(solution)/shard_map/all_to_all | solution.py:214
  63.5 0.1 pieces.1
  63.6 20.4 %all_to_all.20 = f32[64,8,128]{2,1,0:T(8,128)S(1)} all-to-all(f32[64,8,128]{2,1,0:T(8,128)S(1)} %pieces.1), channel_id=1, replica_groups=mesh['z'=8,'y'=8,'x'=4,'c'=2] {'z','y'}, dimensions={0} | all-to-all | bytes 524288 | tf_op jit(solution)/shard_map/all_to_all | solution.py:214
  83.9 0.1 total.1
  84.1 9.0 %all_to_all.21.kept = s16[4,448,128]{2,1,0:T(8,128)(2,1)S(1)} all-to-all(s16[4,448,128]{2,1,0:T(8,128)(2,1)S(1)} %total.1), channel_id=1, replica_groups=mesh['z'=8,'y'=8,'x'=4,'c'=2] {'x'}, dimensions={0} | all-to-all | bytes 917504 | tf_op jit(solution)/shard_map/all_to_all | solution.py:214
  93.0 7.5 %collective-permute-start.5 = (s16[4,448,128]{2,1,0:T(8,128)(2,1)S(1)}, s16[4,448,128]{2,1,0:T(8,128)(2,1)S(1)}, u32[]{:S(2)}, u32[]{:S(2)}) collective-permute-start(s16[4,448,128]{2,1,0:T(8,128)(2,1)S(1)} %all_to_all.21.kept), channel_id=1, source_target_pairs={{0,1},{1,0},{2,3},{3,2},{4,5},{5,4},{6,7},{7,6},{8,9},{9,8},{10,11... | collective-permute-start | bytes 1376264 | tf_op jit(solution)/shard_map/ppermute | solution.py:210
  100.5 0.9 finish.1
  101.5 0.5 collective-permute-done.5.received
  102.0 1.3 %whole.1 = f32[3456,128]{1,0:T(8,128)} custom-call(s16[4,448,128]{2,1,0:T(8,128)(2,1)S(1)} %all_to_all.21.kept, s16[4,448,128]{2,1,0:T(8,128)(2,1)S(1)} %collective-permute-done.5.received), custom_call_target="tpu_custom_call" | custom-call | tf_op jit(solution)/shard_map/whole/pallas_call | solution.py:284
  (5 shorter events, 0.0 us)
Async XLA Ops:
  0.6 10.6 %copy-start.2 = (bf16[1,512,128]{2,1,0:T(8,128)(2,1)S(1)}, bf16[1,512,128]{2,1,0:T(8,128)(2,1)}, u32[]{:S(2)}) copy-start(bf16[1,512,128]{2,1,0:T(8,128)(2,1)} %param.11) | copy-start | bytes 393220
  2.6 7.6 %collective-permute-start = (bf16[128,128]{1,0:T(8,128)(2,1)S(1)}, bf16[128,128]{1,0:T(8,128)(2,1)S(1)}, u32[]{:S(2)}, u32[]{:S(2)}) collective-permute-start(bf16[128,128]{1,0:T(8,128)(2,1)S(1)} %get-tuple-element.23), channel_id=1, source_target_pairs={{0,8},{8,16},{16,24},{24,32},{32,40},{40,48},{48,56},{56,64},{64,7... | collective-permute-start | bytes 98312 | tf_op jit(solution)/shard_map/ppermute | solution.py:233
  6.6 4.7 %collective-permute-start.1 = (bf16[128,128]{1,0:T(8,128)(2,1)S(1)}, bf16[128,128]{1,0:T(8,128)(2,1)S(1)}, u32[]{:S(2)}, u32[]{:S(2)}) collective-permute-start(bf16[128,128]{1,0:T(8,128)(2,1)S(1)} %get-tuple-element.24), channel_id=1, source_target_pairs={{8,0},{16,8},{24,16},{32,24},{40,32},{48,40},{56,48},{64,56},{72,6... | collective-permute-start | bytes 98312 | tf_op jit(solution)/shard_map/ppermute | solution.py:234
  10.1 10.5 %copy-start = (bf16[27,128,128]{2,1,0:T(8,128)(2,1)S(1)}, bf16[27,128,128]{2,1,0:T(8,128)(2,1)}, u32[]{:S(2)}) copy-start(bf16[27,128,128]{2,1,0:T(8,128)(2,1)} %weights.5) | copy-start | bytes 2654212
  13.4 9.7 %collective-permute-start.2 = (f32[1728,128]{1,0:T(8,128)S(1)}, f32[1728,128]{1,0:T(8,128)S(1)}, u32[]{:S(2)}, u32[]{:S(2)}) collective-permute-start(f32[1728,128]{1,0:T(8,128)S(1)} %get-tuple-element.27), channel_id=1, source_target_pairs={{0,1},{1,0},{2,3},{3,2},{4,5},{5,4},{6,7},{7,6},{8,9},{9,8},{10,11... | collective-permute-start | bytes 2654216 | tf_op jit(solution)/shard_map/ppermute | solution.py:210
  24.1 12.4 %all-to-all-start = ((s16[4,448,128]{2,1,0:T(8,128)(2,1)}), s16[4,448,128]{2,1,0:T(8,128)(2,1)S(1)}, u32[]{:S(2)}, u32[]{:S(2)}) async-start(s16[4,448,128]{2,1,0:T(8,128)(2,1)} %halves.1), calls=%async_computation | async-start | bytes 917504 | tf_op jit(solution)/shard_map/all_to_all | solution.py:214
  33.8 66.7 %copy-start.1 = (s32[1,2,128]{2,1,0:T(2,128)S(1)}, s32[1,2,128]{2,1,0:T(2,128)}, u32[]{:S(2)}) copy-start(s32[1,2,128]{2,1,0:T(2,128)} %param.9) | copy-start | bytes 3076
  37.3 26.2 %all-to-all-start.1 = ((f32[64,8,128]{2,1,0:T(8,128)}), f32[64,8,128]{2,1,0:T(8,128)S(1)}, u32[]{:S(2)}, u32[]{:S(2)}) async-start(f32[64,8,128]{2,1,0:T(8,128)} %bitcast.5), calls=%async_computation.1 | async-start | bytes 524288 | tf_op jit(solution)/shard_map/all_to_all | solution.py:214
  50.9 7.2 %collective-permute-start.4 = (f32[128,128]{1,0:T(8,128)S(1)}, f32[128,128]{1,0:T(8,128)S(1)}, u32[]{:S(2)}, u32[]{:S(2)}) collective-permute-start(f32[128,128]{1,0:T(8,128)S(1)} %get-tuple-element.43), channel_id=1, source_target_pairs={{8,0},{16,8},{24,16},{32,24},{40,32},{48,40},{56,48},{64,56},{72,6... | collective-permute-start | bytes 196616 | tf_op jit(solution)/shard_map/ppermute | solution.py:269
  52.2 5.9 %collective-permute-start.3 = (f32[128,128]{1,0:T(8,128)S(1)}, f32[128,128]{1,0:T(8,128)S(1)}, u32[]{:S(2)}, u32[]{:S(2)}) collective-permute-start(f32[128,128]{1,0:T(8,128)S(1)} %get-tuple-element.44), channel_id=1, source_target_pairs={{0,8},{8,16},{16,24},{24,32},{32,40},{40,48},{48,56},{56,64},{64,7... | collective-permute-start | bytes 196616 | tf_op jit(solution)/shard_map/ppermute | solution.py:268
  93.0 8.9 %collective-permute-start.5 = (s16[4,448,128]{2,1,0:T(8,128)(2,1)S(1)}, s16[4,448,128]{2,1,0:T(8,128)(2,1)S(1)}, u32[]{:S(2)}, u32[]{:S(2)}) collective-permute-start(s16[4,448,128]{2,1,0:T(8,128)(2,1)S(1)} %all_to_all.21.kept), channel_id=1, source_target_pairs={{0,1},{1,0},{2,3},{3,2},{4,5},{5,4},{6,7},{7,6},{8,9},{9,8},{10,11... | collective-permute-start | bytes 1376264 | tf_op jit(solution)/shard_map/ppermute | solution.py:210

commit v4 on v3

--- a/solution.py
+++ b/solution.py
@@ -16,6 +16,7 @@
 HALF = KV * C // 2
 QUARTER = HALF // 4
 CODED = QUARTER + 16
+PIECES = 64
 GROUP = 3
 FIRST = 3
 TILE = 256
@@ -128,11 +129,18 @@
     grad_features[...] = masked(count, total).astype(bf16)
 
 
+def exponents(top):
+    return jnp.clip(jnp.floor(jnp.log2(jnp.maximum(top, 1e-37))), -100.0, 100.0)
+
+
+def steps(values, exponent):
+    scaled = jnp.round(values * jnp.exp2(14.0 - exponent))
+    return jnp.clip(scaled, -32767.0, 32767.0).astype(jnp.int32)
+
+
 def encode(values, coded):
-    top = jnp.max(jnp.abs(values), axis=0, keepdims=True)
-    exponent = jnp.clip(jnp.floor(jnp.log2(jnp.maximum(top, 1e-37))), -100.0, 100.0)
-    steps = jnp.round(values * jnp.exp2(14.0 - exponent))
-    coded[:QUARTER, :] = jnp.clip(steps, -32767.0, 32767.0).astype(jnp.int32).astype(jnp.int16)
+    exponent = exponents(jnp.max(jnp.abs(values), axis=0, keepdims=True))
+    coded[:QUARTER, :] = steps(values, exponent).astype(jnp.int16)
     exponent = jnp.broadcast_to(exponent, (CODED - QUARTER, C))
     coded[QUARTER:, :] = exponent.astype(jnp.int32).astype(jnp.int16)
 
@@ -140,6 +148,11 @@
 def decode(coded):
     values = coded[...].astype(jnp.int32).astype(f32)
     return values[:QUARTER, :] * jnp.exp2(values[QUARTER : QUARTER + 1, :] - 14.0)
+
+
+def decode_pieces(coded):
+    values = coded[...].astype(jnp.int32).astype(f32).reshape(PIECES, 8, C)
+    return values * jnp.exp2(values[:, 7:, :] - 14.0)
 
 
 def halves_kernel(kept, received, quarters):
@@ -148,27 +161,38 @@
         encode(kept[rows, :] + received[rows, :], quarters.at[i])
 
 
-def quarters_kernel(quarters, total):
-    total[:QUARTER, :] = sum(decode(quarters.at[i]) for i in range(4))
-    total[QUARTER:, :] = jnp.zeros_like(total[QUARTER:, :])
+def quarters_kernel(quarters, pieces, lines):
+    total = sum(decode(quarters.at[i]) for i in range(4))
+    total = jnp.concatenate([total, jnp.zeros((7 * PIECES - QUARTER, C), f32)], axis=0)
+    parts = [total[j * PIECES : (j + 1) * PIECES, :] for j in range(7)]
+    exponent = exponents(functools.reduce(jnp.maximum, [jnp.abs(part) for part in parts]))
+    for j, part in enumerate(parts):
+        lines[pl.ds(j, PIECES, stride=8), :] = steps(part, exponent)
+    lines[pl.ds(7, PIECES, stride=8), :] = exponent.astype(jnp.int32)
+    pieces[...] = lines[...].astype(jnp.int16)
 
 
 def pieces_kernel(pieces, spread):
-    spread[...] = jnp.broadcast_to(jnp.sum(pieces[...], axis=0)[None], spread.shape)
-
-
-def total_kernel(total, quarters):
-    encode(total[:QUARTER, :], quarters.at[0])
-    for i in range(1, 4):
-        quarters[i] = quarters[0]
-
-
-def whole_kernel(kept, received, whole, buffer, sems):
+    total = jnp.sum(decode_pieces(pieces), axis=0)
+    last = lax.broadcasted_iota(jnp.int32, total.shape, 0) == 7
+    total = jnp.where(last, 0.0, total)
+    exponent = exponents(jnp.max(jnp.abs(total), axis=0, keepdims=True))
+    coded = jnp.where(last, exponent.astype(jnp.int32), steps(total, exponent))
+    coded = jnp.broadcast_to(coded[None], (PIECES, 8, C)).reshape(8 * PIECES, C)
+    spread[...] = coded.astype(jnp.int16)
+
+
+def whole_kernel(kept, received, whole, lines, buffer, sems):
     core = lax.axis_index("c")
     copies = []
     for i, (half, place) in enumerate(((kept, core), (received, 1 - core))):
-        for j in range(4):
-            buffer[i, j * QUARTER : (j + 1) * QUARTER, :] = decode(half.at[j])
+        for q in range(4):
+            lines[4 * i + q] = decode_pieces(half.at[q]).reshape(8 * PIECES, C)
+            for j in range(7):
+                start = j * PIECES
+                count = min(PIECES, QUARTER - start)
+                rows = slice(q * QUARTER + start, q * QUARTER + start + count)
+                buffer[i, rows, :] = lines[4 * i + q, pl.ds(j, count, stride=8), :]
         rows = pl.ds(pl.multiple_of(place * HALF, 8), HALF)
         copies.append(pltpu.make_async_copy(buffer.at[i], whole.at[rows], sems.at[i]))
         copies[i].start()
@@ -263,15 +287,23 @@
     quarters = exchange(quarters, "x")
     ext_grad = scatter("scatter_rest", (FIRST, KV), (grad_rows, weights, kernel_map, ext_grad))
     quarters, ext_grad = lax.optimization_barrier((quarters, ext_grad))
-    (total,) = call(quarters_kernel, "quarters", (quarters,), [((VOX, C), f32)], scalars=0)
-    pieces = exchange(total.reshape(size, -1, C), space)
+    dealt = ((8 * PIECES, C), jnp.int16)
+    (pieces,) = call(
+        quarters_kernel,
+        "quarters",
+        (quarters,),
+        [dealt],
+        [((8 * PIECES, C), jnp.int32)],
+        scalars=0,
+    )
+    pieces = exchange(pieces.reshape(PIECES, 8, C), space)
     for_lower = lax.ppermute(ext_grad[VOX + HALO :], space, up)
     for_upper = lax.ppermute(ext_grad[VOX : VOX + HALO], space, down)
     pieces, for_lower, for_upper = lax.optimization_barrier((pieces, for_lower, for_upper))
-    (pieces,) = call(pieces_kernel, "pieces", (pieces,), [((size, 8, C), f32)], scalars=0)
-    total = exchange(pieces, space).reshape(VOX, C)
-    (quarters,) = call(total_kernel, "total", (total,), [coded], scalars=0)
-    half = exchange(quarters, "x")
+    pieces = pieces.reshape(8 * PIECES, C)
+    (pieces,) = call(pieces_kernel, "pieces", (pieces,), [dealt], scalars=0)
+    quarter = exchange(pieces.reshape(PIECES, 8, C), space).reshape(8 * PIECES, C)
+    half = exchange(jnp.broadcast_to(quarter[None], (4, 8 * PIECES, C)), "x")
     half, ext_grad = lax.optimization_barrier((half, ext_grad))
     received = across_c(half)
     (grad_features,) = call(
@@ -287,7 +319,11 @@
         in_specs=[pl.BlockSpec(memory_space=pltpu.VMEM)] * 2,
         out_specs=pl.BlockSpec(memory_space=pl.ANY),
         out_shape=jax.ShapeDtypeStruct((KV * C, C), f32),
-        scratch_shapes=[pltpu.VMEM((2, HALF, C), f32), pltpu.SemaphoreType.DMA((2,))],
+        scratch_shapes=[
+            pltpu.VMEM((8, 8 * PIECES, C), f32),
+            pltpu.VMEM((2, HALF, C), f32),
+            pltpu.SemaphoreType.DMA((2,)),
+        ],
         compiler_params=pltpu.CompilerParams(vmem_limit_bytes=8 * 2**20),
     )(half, received).reshape(KV, C, C)
     return output[None], grad_features[None], grad_weights

time: 104 us -> 104 us (level)
    pallas_call x11 -> x10, Pallas kernels: 17 us -> 17.1 us  [call(): pl.pallas_call(kernel, name=name, in_specs=[scalar] * scalars + [operand]...]
  transfers between devices with their start and end apart: 8 -> 8, of which waited for: 5 -> 6; matrix products, arithmetic and copies ran while one was open for 0% -> 0% of each run, Pallas kernels for 11% -> 11%
where the time goes in v4:
time: 104 us; the launch traced here: 103 us
  starting transfers between devices  42.6 us (41%)
  blocking collectives  29.7 us (29%)
  Pallas kernels  18.7 us (18%)
  waiting for transfers between devices  10.6 us (10%)
  between operations  1.66 us (2%)
    all_to_all x2, blocking collectives, exchange(): return lax.all_to_all(pieces, axes, 0, 0, tiled=False)  29.7 us
    all_to_all x2, starting transfers between devices, exchange(): return lax.all_to_all(pieces, axes, 0, 0, tiled=False)  17.2 us
    pallas_call x10, Pallas kernels, call(): pl.pallas_call(kernel, name=name, in_specs=[scalar] * scalars + [operand]...  17.1 us
    ppermute x2, starting transfers between devices, across_c(): return lax.ppermute(part, 'c', [(0, 1), (1, 0)])  14.7 us
    all_to_all x2, waiting for transfers between devices, exchange(): return lax.all_to_all(pieces, axes, 0, 0, tiled=False)  7.62 us
    ppermute x1, starting transfers between devices, per_device(): lower_in = lax.ppermute(to_upper, space, up)  4.03 us
    ppermute x1, starting transfers between devices, per_device(): for_lower = lax.ppermute(ext_grad[VOX + HALO:], space, up)  3.99 us
  transfers between devices with their start and end apart: 8, of which 6 were waited for; matrix products, arithmetic and copies ran while one was open for 0% of the time, Pallas kernels for 11%

profile of v4, /device:TPU:1, one launch (start us, length us, event | category | flops | bytes accessed | tf_op | source)
XLA Modules:
  0.0 103.4 jit_solution(6694233537665902456)
XLA Ops:
  1.3 1.2 %pick.1 = (bf16[128,128]{1,0:T(8,128)(2,1)S(1)}, bf16[128,128]{1,0:T(8,128)(2,1)S(1)}, bf16[128,512]{1,0:T(8,128)(2,1)S(1)}, s32[27,1,512]{2,1,0:T(1,128)S(1)}) custom-call(s32[1,1]{1,0:T(1,128)S(6)} %copy.9.count, bf16[512,128]{1,0:T(8,128)(2,1)} %bitcast.19, s32[2,128]{1,0:T(2,128)} %bitcast.13, s32[27,1,512]{2,1,0:T(1,128)} %bitcast.21), custom_call_target="tpu_custom_call" | custom-call | bytes 439300 | tf_op jit(solution)/shard_map/pick/pallas_call | solution.py:209
  2.6 4.0 %collective-permute-start = (bf16[128,128]{1,0:T(8,128)(2,1)S(1)}, bf16[128,128]{1,0:T(8,128)(2,1)S(1)}, u32[]{:S(2)}, u32[]{:S(2)}) collective-permute-start(bf16[128,128]{1,0:T(8,128)(2,1)S(1)} %get-tuple-element.23), channel_id=1, source_target_pairs={{0,8},{8,16},{16,24},{24,32},{32,40},{40,48},{48,56},{56,64},{64,7... | collective-permute-start | bytes 98312 | tf_op jit(solution)/shard_map/ppermute | solution.py:257
  6.6 1.3 %collective-permute-start.1 = (bf16[128,128]{1,0:T(8,128)(2,1)S(1)}, bf16[128,128]{1,0:T(8,128)(2,1)S(1)}, u32[]{:S(2)}, u32[]{:S(2)}) collective-permute-start(bf16[128,128]{1,0:T(8,128)(2,1)S(1)} %get-tuple-element.24), channel_id=1, source_target_pairs={{8,0},{16,8},{24,16},{32,24},{40,32},{48,40},{56,48},{64,56},{72,6... | collective-permute-start | bytes 98312 | tf_op jit(solution)/shard_map/ppermute | solution.py:258
  7.9 2.2 %local.1.own = bf16[3456,512]{1,0:T(8,128)(2,1)S(1)} custom-call(bf16[128,512]{1,0:T(8,128)(2,1)S(1)} %get-tuple-element.26.table, s32[27,1,512]{2,1,0:T(1,128)S(1)} %get-tuple-element.25.kernel_map), custom_call_target="tpu_custom_call" | custom-call | flops 1811939328 | bytes 3725312 | tf_op jit(solution)/shard_map/local/pallas_call | solution.py:209
  10.1 0.0 copy-start
  10.1 0.0 collective-permute-done.lower
  10.1 1.1 %collective-permute-done.1.upper = bf16[128,128]{1,0:T(8,128)(2,1)S(1)} collective-permute-done((bf16[128,128]{1,0:T(8,128)(2,1)S(1)}, bf16[128,128]{1,0:T(8,128)(2,1)S(1)}, u32[]{:S(2)}, u32[]{:S(2)}) %collective-permute-start.1) | collective-permute-done | bytes 32800 | tf_op jit(solution)/shard_map/ppermute | solution.py:258
  11.3 2.2 %halo.1 = (f32[1728,128]{1,0:T(8,128)S(1)}, f32[1728,128]{1,0:T(8,128)S(1)}, bf16[3456,512]{1,0:T(8,128)(2,1)S(1)}, bf16[512,128]{1,0:T(8,128)(2,1)S(1)}) custom-call(s32[1,1]{1,0:T(1,128)S(6)} %copy.9.count, bf16[128,128]{1,0:T(8,128)(2,1)S(1)} %collective-permute-done.lower, bf16[128,128]{1,0:T(8,128)(2,1)S(1)} %collective-permute-done.1.upper, ...), custom_call_target="tpu_custom_call" | custom-call | flops 1358954496 | bytes 9230340 | tf_op jit(solution)/shard_map/halo/pallas_call | solution.py:209
  13.5 7.2 %collective-permute-start.2 = (f32[1728,128]{1,0:T(8,128)S(1)}, f32[1728,128]{1,0:T(8,128)S(1)}, u32[]{:S(2)}, u32[]{:S(2)}) collective-permute-start(f32[1728,128]{1,0:T(8,128)S(1)} %get-tuple-element.27), channel_id=1, source_target_pairs={{0,1},{1,0},{2,3},{3,2},{4,5},{5,4},{6,7},{7,6},{8,9},{9,8},{10,11... | collective-permute-start | bytes 2654216 | tf_op jit(solution)/shard_map/ppermute | solution.py:234
  20.7 1.4 %output.1 = bf16[512,128]{1,0:T(8,128)(2,1)} custom-call(s32[1,1]{1,0:T(1,128)S(6)} %copy.9.count, bf16[27,128,128]{2,1,0:T(8,128)(2,1)S(1)} %copy-done, bf16[3456,512]{1,0:T(8,128)(2,1)S(1)} %get-tuple-element.29.gathered), custom_call_target="tpu_custom_call" | custom-call | flops 452984832 | bytes 4554756 | tf_op jit(solution)/shard_map/output/pallas_call | solution.py:209
  22.1 1.0 %scatter_first.1.refs_0_ = f32[768,128]{1,0:T(8,128)S(1)} custom-call(bf16[512,128]{1,0:T(8,128)(2,1)S(1)} %get-tuple-element.28.grad_rows, bf16[27,128,128]{2,1,0:T(8,128)(2,1)S(1)} %copy-done, s32[27,1,512]{2,1,0:T(1,128)S(1)} %get-tuple-element.25.kernel_map), custom_call_target="tpu_custom_call" | custom-call | flops 654311424 | bytes 1464320 | tf_op jit(solution)/shard_map/scatter_first/pallas_call | solution.py:209
  23.1 0.0 collective-permute-done.2.received
  23.1 1.0 halves.1
  24.2 3.6 %all-to-all-start = ((s16[4,448,128]{2,1,0:T(8,128)(2,1)}), s16[4,448,128]{2,1,0:T(8,128)(2,1)S(1)}, u32[]{:S(2)}, u32[]{:S(2)}) async-start(s16[4,448,128]{2,1,0:T(8,128)(2,1)} %halves.1), calls=%async_computation | async-start | bytes 917504 | tf_op jit(solution)/shard_map/all_to_all | solution.py:238
  27.8 0.0 copy-start.1
  27.8 6.0 %scatter_rest.1.ext_grad = f32[768,128]{1,0:T(8,128)S(1)} custom-call(bf16[512,128]{1,0:T(8,128)(2,1)S(1)} %get-tuple-element.28.grad_rows, bf16[27,128,128]{2,1,0:T(8,128)(2,1)S(1)} %copy-done, s32[27,1,512]{2,1,0:T(1,128)S(1)} %get-tuple-element.25.kernel_map, f32[768,128]{1,0:T(8,128)S(1)} %scatter_first.1.refs_0_), custom_call_target="tpu_custom_call" | custom-call | flops 5234491392 | bytes 1857536 | tf_op jit(solution)/shard_map/scatter_rest/pallas_call | solution.py:209
  33.9 2.7 %all-to-all-done.quarters = s16[4,448,128]{2,1,0:T(8,128)(2,1)S(1)} async-done(((s16[4,448,128]{2,1,0:T(8,128)(2,1)}), s16[4,448,128]{2,1,0:T(8,128)(2,1)S(1)}, u32[]{:S(2)}, u32[]{:S(2)}) %all-to-all-start) | async-done | bytes 458784 | tf_op jit(solution)/shard_map/all_to_all | solution.py:238
  36.5 0.9 quarters.1
  37.4 13.6 %all-to-all-start.1 = ((s16[64,8,128]{2,1,0:T(8,128)(2,1)}), s16[64,8,128]{2,1,0:T(8,128)(2,1)S(1)}, u32[]{:S(2)}, u32[]{:S(2)}) async-start(s16[64,8,128]{2,1,0:T(8,128)(2,1)} %bitcast.5), calls=%async_computation.1 | async-start | bytes 262144 | tf_op jit(solution)/shard_map/all_to_all | solution.py:238
  51.1 1.3 %collective-permute-start.4 = (f32[128,128]{1,0:T(8,128)S(1)}, f32[128,128]{1,0:T(8,128)S(1)}, u32[]{:S(2)}, u32[]{:S(2)}) collective-permute-start(f32[128,128]{1,0:T(8,128)S(1)} %get-tuple-element.43), channel_id=1, source_target_pairs={{8,0},{16,8},{24,16},{32,24},{40,32},{48,40},{56,48},{64,56},{72,6... | collective-permute-start | bytes 196616 | tf_op jit(solution)/shard_map/ppermute | solution.py:301
  52.4 4.0 %collective-permute-start.3 = (f32[128,128]{1,0:T(8,128)S(1)}, f32[128,128]{1,0:T(8,128)S(1)}, u32[]{:S(2)}, u32[]{:S(2)}) collective-permute-start(f32[128,128]{1,0:T(8,128)S(1)} %get-tuple-element.44), channel_id=1, source_target_pairs={{0,8},{8,16},{16,24},{24,32},{32,40},{40,48},{48,56},{56,64},{64,7... | collective-permute-start | bytes 196616 | tf_op jit(solution)/shard_map/ppermute | solution.py:300
  56.4 0.9 collective-permute-done.4.for_upper
  57.3 0.4 collective-permute-done.3.for_lower
  57.7 5.0 %all-to-all-done.1 = s16[64,8,128]{2,1,0:T(8,128)(2,1)S(1)} async-done(((s16[64,8,128]{2,1,0:T(8,128)(2,1)}), s16[64,8,128]{2,1,0:T(8,128)(2,1)S(1)}, u32[]{:S(2)}, u32[]{:S(2)}) %all-to-all-start.1) | async-done | bytes 131104 | tf_op jit(solution)/shard_map/all_to_all | solution.py:238
  62.6 0.1 pieces.1
  62.8 20.4 %all_to_all.20 = s16[64,8,128]{2,1,0:T(8,128)(2,1)S(1)} all-to-all(s16[64,8,128]{2,1,0:T(8,128)(2,1)S(1)} %bitcast.12), channel_id=1, replica_groups=mesh['z'=8,'y'=8,'x'=4,'c'=2] {'z','y'}, dimensions={0} | all-to-all | bytes 262144 | tf_op jit(solution)/shard_map/all_to_all | solution.py:238
  83.1 0.1 broadcast_in_dim.15
  83.2 9.3 %all_to_all.21.kept = s16[4,512,128]{2,1,0:T(8,128)(2,1)S(1)} all-to-all(s16[4,512,128]{2,1,0:T(8,128)(2,1)S(1)} %broadcast_in_dim.15), channel_id=1, replica_groups=mesh['z'=8,'y'=8,'x'=4,'c'=2] {'x'}, dimensions={0} | all-to-all | bytes 1048576 | tf_op jit(solution)/shard_map/all_to_all | solution.py:238
  92.5 7.5 %collective-permute-start.5 = (s16[4,512,128]{2,1,0:T(8,128)(2,1)S(1)}, s16[4,512,128]{2,1,0:T(8,128)(2,1)S(1)}, u32[]{:S(2)}, u32[]{:S(2)}) collective-permute-start(s16[4,512,128]{2,1,0:T(8,128)(2,1)S(1)} %all_to_all.21.kept), channel_id=1, source_target_pairs={{0,1},{1,0},{2,3},{3,2},{4,5},{5,4},{6,7},{7,6},{8,9},{9,8},{10,11... | collective-permute-start | bytes 1572872 | tf_op jit(solution)/shard_map/ppermute | solution.py:234
  100.1 0.9 finish.1
  101.0 0.6 collective-permute-done.5.received
  101.6 1.6 %whole.1 = f32[3456,128]{1,0:T(8,128)} custom-call(s16[4,512,128]{2,1,0:T(8,128)(2,1)S(1)} %all_to_all.21.kept, s16[4,512,128]{2,1,0:T(8,128)(2,1)S(1)} %collective-permute-done.5.received), custom_call_target="tpu_custom_call" | custom-call | tf_op jit(solution)/shard_map/whole/pallas_call | solution.py:316
  (5 shorter events, 0.0 us)
Async XLA Ops:
  0.6 10.6 %copy-start.2 = (bf16[1,512,128]{2,1,0:T(8,128)(2,1)S(1)}, bf16[1,512,128]{2,1,0:T(8,128)(2,1)}, u32[]{:S(2)}) copy-start(bf16[1,512,128]{2,1,0:T(8,128)(2,1)} %param.11) | copy-start | bytes 393220
  2.6 7.6 %collective-permute-start = (bf16[128,128]{1,0:T(8,128)(2,1)S(1)}, bf16[128,128]{1,0:T(8,128)(2,1)S(1)}, u32[]{:S(2)}, u32[]{:S(2)}) collective-permute-start(bf16[128,128]{1,0:T(8,128)(2,1)S(1)} %get-tuple-element.23), channel_id=1, source_target_pairs={{0,8},{8,16},{16,24},{24,32},{32,40},{40,48},{48,56},{56,64},{64,7... | collective-permute-start | bytes 98312 | tf_op jit(solution)/shard_map/ppermute | solution.py:257
  6.6 4.7 %collective-permute-start.1 = (bf16[128,128]{1,0:T(8,128)(2,1)S(1)}, bf16[128,128]{1,0:T(8,128)(2,1)S(1)}, u32[]{:S(2)}, u32[]{:S(2)}) collective-permute-start(bf16[128,128]{1,0:T(8,128)(2,1)S(1)} %get-tuple-element.24), channel_id=1, source_target_pairs={{8,0},{16,8},{24,16},{32,24},{40,32},{48,40},{56,48},{64,56},{72,6... | collective-permute-start | bytes 98312 | tf_op jit(solution)/shard_map/ppermute | solution.py:258
  10.1 10.5 %copy-start = (bf16[27,128,128]{2,1,0:T(8,128)(2,1)S(1)}, bf16[27,128,128]{2,1,0:T(8,128)(2,1)}, u32[]{:S(2)}) copy-start(bf16[27,128,128]{2,1,0:T(8,128)(2,1)} %weights.5) | copy-start | bytes 2654212
  13.5 9.7 %collective-permute-start.2 = (f32[1728,128]{1,0:T(8,128)S(1)}, f32[1728,128]{1,0:T(8,128)S(1)}, u32[]{:S(2)}, u32[]{:S(2)}) collective-permute-start(f32[1728,128]{1,0:T(8,128)S(1)} %get-tuple-element.27), channel_id=1, source_target_pairs={{0,1},{1,0},{2,3},{3,2},{4,5},{5,4},{6,7},{7,6},{8,9},{9,8},{10,11... | collective-permute-start | bytes 2654216 | tf_op jit(solution)/shard_map/ppermute | solution.py:234
  24.2 12.4 %all-to-all-start = ((s16[4,448,128]{2,1,0:T(8,128)(2,1)}), s16[4,448,128]{2,1,0:T(8,128)(2,1)S(1)}, u32[]{:S(2)}, u32[]{:S(2)}) async-start(s16[4,448,128]{2,1,0:T(8,128)(2,1)} %halves.1), calls=%async_computation | async-start | bytes 917504 | tf_op jit(solution)/shard_map/all_to_all | solution.py:238
  27.8 72.3 %copy-start.1 = (s32[1,2,128]{2,1,0:T(2,128)S(1)}, s32[1,2,128]{2,1,0:T(2,128)}, u32[]{:S(2)}) copy-start(s32[1,2,128]{2,1,0:T(2,128)} %param.9) | copy-start | bytes 3076
  37.4 25.2 %all-to-all-start.1 = ((s16[64,8,128]{2,1,0:T(8,128)(2,1)}), s16[64,8,128]{2,1,0:T(8,128)(2,1)S(1)}, u32[]{:S(2)}, u32[]{:S(2)}) async-start(s16[64,8,128]{2,1,0:T(8,128)(2,1)} %bitcast.5), calls=%async_computation.1 | async-start | bytes 262144 | tf_op jit(solution)/shard_map/all_to_all | solution.py:238
  51.1 6.2 %collective-permute-start.4 = (f32[128,128]{1,0:T(8,128)S(1)}, f32[128,128]{1,0:T(8,128)S(1)}, u32[]{:S(2)}, u32[]{:S(2)}) collective-permute-start(f32[128,128]{1,0:T(8,128)S(1)} %get-tuple-element.43), channel_id=1, source_target_pairs={{8,0},{16,8},{24,16},{32,24},{40,32},{48,40},{56,48},{64,56},{72,6... | collective-permute-start | bytes 196616 | tf_op jit(solution)/shard_map/ppermute | solution.py:301
  52.4 5.3 %collective-permute-start.3 = (f32[128,128]{1,0:T(8,128)S(1)}, f32[128,128]{1,0:T(8,128)S(1)}, u32[]{:S(2)}, u32[]{:S(2)}) collective-permute-start(f32[128,128]{1,0:T(8,128)S(1)} %get-tuple-element.44), channel_id=1, source_target_pairs={{0,8},{8,16},{16,24},{24,32},{32,40},{40,48},{48,56},{56,64},{64,7... | collective-permute-start | bytes 196616 | tf_op jit(solution)/shard_map/ppermute | solution.py:300
  92.5 9.1 %collective-permute-start.5 = (s16[4,512,128]{2,1,0:T(8,128)(2,1)S(1)}, s16[4,512,128]{2,1,0:T(8,128)(2,1)S(1)}, u32[]{:S(2)}, u32[]{:S(2)}) collective-permute-start(s16[4,512,128]{2,1,0:T(8,128)(2,1)S(1)} %all_to_all.21.kept), channel_id=1, source_target_pairs={{0,1},{1,0},{2,3},{3,2},{4,5},{5,4},{6,7},{7,6},{8,9},{9,8},{10,11... | collective-permute-start | bytes 1572872 | tf_op jit(solution)/shard_map/ppermute | solution.py:234

commit v5 on v4

--- a/solution.py
+++ b/solution.py
@@ -297,12 +297,13 @@
         scalars=0,
     )
     pieces = exchange(pieces.reshape(PIECES, 8, C), space)
-    for_lower = lax.ppermute(ext_grad[VOX + HALO :], space, up)
-    for_upper = lax.ppermute(ext_grad[VOX : VOX + HALO], space, down)
-    pieces, for_lower, for_upper = lax.optimization_barrier((pieces, for_lower, for_upper))
+    pieces, ext_grad = lax.optimization_barrier((pieces, ext_grad))
     pieces = pieces.reshape(8 * PIECES, C)
     (pieces,) = call(pieces_kernel, "pieces", (pieces,), [dealt], scalars=0)
     quarter = exchange(pieces.reshape(PIECES, 8, C), space).reshape(8 * PIECES, C)
+    for_lower = lax.ppermute(ext_grad[VOX + HALO :], space, up)
+    for_upper = lax.ppermute(ext_grad[VOX : VOX + HALO], space, down)
+    quarter, for_lower, for_upper = lax.optimization_barrier((quarter, for_lower, for_upper))
     half = exchange(jnp.broadcast_to(quarter[None], (4, 8 * PIECES, C)), "x")
     half, ext_grad = lax.optimization_barrier((half, ext_grad))
     received = across_c(half)

time: 104 us -> 98.7 us (0.949)
  starting transfers between devices: 42.6 us -> 32.9 us
  blocking collectives: 29.7 us -> 34.3 us
    all_to_all x2, starting transfers between devices: 17.2 us -> 8.26 us  [exchange(): return lax.all_to_all(pieces, axes, 0, 0, tiled=False)]
    all_to_all x2, blocking collectives: 29.7 us -> 34.3 us  [exchange(): return lax.all_to_all(pieces, axes, 0, 0, tiled=False)]
  transfers between devices with their start and end apart: 8 -> 8, of which waited for: 6 -> 6; matrix products, arithmetic and copies ran while one was open for 0% -> 0% of each run, Pallas kernels for 11% -> 12%
where the time goes in v5:
time: 98.7 us; the launch traced here: 98.2 us
  blocking collectives  34.3 us (35%)
  starting transfers between devices  32.9 us (33%)
  Pallas kernels  18.7 us (19%)
  waiting for transfers between devices  10.6 us (11%)
  between operations  1.66 us (2%)
    all_to_all x2, blocking collectives, exchange(): return lax.all_to_all(pieces, axes, 0, 0, tiled=False)  34.3 us
    pallas_call x10, Pallas kernels, call(): pl.pallas_call(kernel, name=name, in_specs=[scalar] * scalars + [operand]...  17.1 us
    ppermute x2, starting transfers between devices, across_c(): return lax.ppermute(part, 'c', [(0, 1), (1, 0)])  14 us
    all_to_all x2, starting transfers between devices, exchange(): return lax.all_to_all(pieces, axes, 0, 0, tiled=False)  8.26 us
    all_to_all x2, waiting for transfers between devices, exchange(): return lax.all_to_all(pieces, axes, 0, 0, tiled=False)  7.53 us
    ppermute x1, starting transfers between devices, per_device(): lower_in = lax.ppermute(to_upper, space, up)  4.03 us
    ppermute x1, starting transfers between devices, per_device(): for_lower = lax.ppermute(ext_grad[VOX + HALO:], space, up)  3.99 us
  transfers between devices with their start and end apart: 8, of which 6 were waited for; matrix products, arithmetic and copies ran while one was open for 0% of the time, Pallas kernels for 12%

profile of v5, /device:TPU:1, one launch (start us, length us, event | category | flops | bytes accessed | tf_op | source)
XLA Modules:
  0.0 98.2 jit_solution(11582499292359120453)
XLA Ops:
  1.3 1.2 %pick.1 = (bf16[128,128]{1,0:T(8,128)(2,1)S(1)}, bf16[128,128]{1,0:T(8,128)(2,1)S(1)}, bf16[128,512]{1,0:T(8,128)(2,1)S(1)}, s32[27,1,512]{2,1,0:T(1,128)S(1)}) custom-call(s32[1,1]{1,0:T(1,128)S(6)} %copy.9.count, bf16[512,128]{1,0:T(8,128)(2,1)} %bitcast.19, s32[2,128]{1,0:T(2,128)} %bitcast.13, s32[27,1,512]{2,1,0:T(1,128)} %bitcast.21), custom_call_target="tpu_custom_call" | custom-call | bytes 439300 | tf_op jit(solution)/shard_map/pick/pallas_call | solution.py:209
  2.6 4.0 %collective-permute-start = (bf16[128,128]{1,0:T(8,128)(2,1)S(1)}, bf16[128,128]{1,0:T(8,128)(2,1)S(1)}, u32[]{:S(2)}, u32[]{:S(2)}) collective-permute-start(bf16[128,128]{1,0:T(8,128)(2,1)S(1)} %get-tuple-element.25), channel_id=1, source_target_pairs={{0,8},{8,16},{16,24},{24,32},{32,40},{40,48},{48,56},{56,64},{64,7... | collective-permute-start | bytes 98312 | tf_op jit(solution)/shard_map/ppermute | solution.py:257
  6.6 1.3 %collective-permute-start.1 = (bf16[128,128]{1,0:T(8,128)(2,1)S(1)}, bf16[128,128]{1,0:T(8,128)(2,1)S(1)}, u32[]{:S(2)}, u32[]{:S(2)}) collective-permute-start(bf16[128,128]{1,0:T(8,128)(2,1)S(1)} %get-tuple-element.26), channel_id=1, source_target_pairs={{8,0},{16,8},{24,16},{32,24},{40,32},{48,40},{56,48},{64,56},{72,6... | collective-permute-start | bytes 98312 | tf_op jit(solution)/shard_map/ppermute | solution.py:258
  7.9 2.2 %local.1.own = bf16[3456,512]{1,0:T(8,128)(2,1)S(1)} custom-call(bf16[128,512]{1,0:T(8,128)(2,1)S(1)} %get-tuple-element.28.table, s32[27,1,512]{2,1,0:T(1,128)S(1)} %get-tuple-element.27.kernel_map), custom_call_target="tpu_custom_call" | custom-call | flops 1811939328 | bytes 3725312 | tf_op jit(solution)/shard_map/local/pallas_call | solution.py:209
  10.1 0.0 copy-start
  10.1 0.0 collective-permute-done.lower
  10.1 1.1 %collective-permute-done.1.upper = bf16[128,128]{1,0:T(8,128)(2,1)S(1)} collective-permute-done((bf16[128,128]{1,0:T(8,128)(2,1)S(1)}, bf16[128,128]{1,0:T(8,128)(2,1)S(1)}, u32[]{:S(2)}, u32[]{:S(2)}) %collective-permute-start.1) | collective-permute-done | bytes 32800 | tf_op jit(solution)/shard_map/ppermute | solution.py:258
  11.3 2.2 %halo.1 = (f32[1728,128]{1,0:T(8,128)S(1)}, f32[1728,128]{1,0:T(8,128)S(1)}, bf16[3456,512]{1,0:T(8,128)(2,1)S(1)}, bf16[512,128]{1,0:T(8,128)(2,1)S(1)}) custom-call(s32[1,1]{1,0:T(1,128)S(6)} %copy.9.count, bf16[128,128]{1,0:T(8,128)(2,1)S(1)} %collective-permute-done.lower, bf16[128,128]{1,0:T(8,128)(2,1)S(1)} %collective-permute-done.1.upper, ...), custom_call_target="tpu_custom_call" | custom-call | flops 1358954496 | bytes 9230340 | tf_op jit(solution)/shard_map/halo/pallas_call | solution.py:209
  13.5 7.2 %collective-permute-start.2 = (f32[1728,128]{1,0:T(8,128)S(1)}, f32[1728,128]{1,0:T(8,128)S(1)}, u32[]{:S(2)}, u32[]{:S(2)}) collective-permute-start(f32[1728,128]{1,0:T(8,128)S(1)} %get-tuple-element.29), channel_id=1, source_target_pairs={{0,1},{1,0},{2,3},{3,2},{4,5},{5,4},{6,7},{7,6},{8,9},{9,8},{10,11... | collective-permute-start | bytes 2654216 | tf_op jit(solution)/shard_map/ppermute | solution.py:234
  20.7 1.4 %output.1 = bf16[512,128]{1,0:T(8,128)(2,1)} custom-call(s32[1,1]{1,0:T(1,128)S(6)} %copy.9.count, bf16[27,128,128]{2,1,0:T(8,128)(2,1)S(1)} %copy-done, bf16[3456,512]{1,0:T(8,128)(2,1)S(1)} %get-tuple-element.31.gathered), custom_call_target="tpu_custom_call" | custom-call | flops 452984832 | bytes 4554756 | tf_op jit(solution)/shard_map/output/pallas_call | solution.py:209
  22.1 1.0 %scatter_first.1.refs_0_ = f32[768,128]{1,0:T(8,128)S(1)} custom-call(bf16[512,128]{1,0:T(8,128)(2,1)S(1)} %get-tuple-element.30.grad_rows, bf16[27,128,128]{2,1,0:T(8,128)(2,1)S(1)} %copy-done, s32[27,1,512]{2,1,0:T(1,128)S(1)} %get-tuple-element.27.kernel_map), custom_call_target="tpu_custom_call" | custom-call | flops 654311424 | bytes 1464320 | tf_op jit(solution)/shard_map/scatter_first/pallas_call | solution.py:209
  23.1 0.0 collective-permute-done.2.received
  23.1 1.0 %halves.1 = s16[4,448,128]{2,1,0:T(8,128)(2,1)} custom-call(f32[1728,128]{1,0:T(8,128)S(1)} %get-tuple-element.33.kept, f32[1728,128]{1,0:T(8,128)S(1)} %collective-permute-done.2.received), custom_call_target="tpu_custom_call" | custom-call | bytes 2228224 | tf_op jit(solution)/shard_map/halves/pallas_call | solution.py:209
  24.2 3.6 %all-to-all-start = ((s16[4,448,128]{2,1,0:T(8,128)(2,1)}), s16[4,448,128]{2,1,0:T(8,128)(2,1)S(1)}, u32[]{:S(2)}, u32[]{:S(2)}) async-start(s16[4,448,128]{2,1,0:T(8,128)(2,1)} %halves.1), calls=%async_computation | async-start | bytes 917504 | tf_op jit(solution)/shard_map/all_to_all | solution.py:238
  27.8 0.0 copy-start.1
  27.8 6.0 %scatter_rest.1.ext_grad = f32[768,128]{1,0:T(8,128)S(1)} custom-call(bf16[512,128]{1,0:T(8,128)(2,1)S(1)} %get-tuple-element.30.grad_rows, bf16[27,128,128]{2,1,0:T(8,128)(2,1)S(1)} %copy-done, s32[27,1,512]{2,1,0:T(1,128)S(1)} %get-tuple-element.27.kernel_map, f32[768,128]{1,0:T(8,128)S(1)} %scatter_first.1.refs_0_), custom_call_target="tpu_custom_call" | custom-call | flops 5234491392 | bytes 1857536 | tf_op jit(solution)/shard_map/scatter_rest/pallas_call | solution.py:209
  33.9 2.7 %all-to-all-done.quarters = s16[4,448,128]{2,1,0:T(8,128)(2,1)S(1)} async-done(((s16[4,448,128]{2,1,0:T(8,128)(2,1)}), s16[4,448,128]{2,1,0:T(8,128)(2,1)S(1)}, u32[]{:S(2)}, u32[]{:S(2)}) %all-to-all-start) | async-done | bytes 458784 | tf_op jit(solution)/shard_map/all_to_all | solution.py:238
  36.5 0.2 quarters.1
  36.8 25.0 %all_to_all.20 = s16[64,8,128]{2,1,0:T(8,128)(2,1)S(1)} all-to-all(s16[64,8,128]{2,1,0:T(8,128)(2,1)S(1)} %bitcast.12), channel_id=1, replica_groups=mesh['z'=8,'y'=8,'x'=4,'c'=2] {'z','y'}, dimensions={0} | all-to-all | bytes 262144 | tf_op jit(solution)/shard_map/all_to_all | solution.py:238
  61.8 0.8 pieces.1
  62.5 4.6 %all-to-all-start.2 = ((s16[64,8,128]{2,1,0:T(8,128)(2,1)}), s16[64,8,128]{2,1,0:T(8,128)(2,1)S(1)}, u32[]{:S(2)}, u32[]{:S(2)}) async-start(s16[64,8,128]{2,1,0:T(8,128)(2,1)} %bitcast.7), calls=%async_computation.2 | async-start | bytes 262144 | tf_op jit(solution)/shard_map/all_to_all | solution.py:238
  67.2 1.3 %collective-permute-start.4 = (f32[128,128]{1,0:T(8,128)S(1)}, f32[128,128]{1,0:T(8,128)S(1)}, u32[]{:S(2)}, u32[]{:S(2)}) collective-permute-start(f32[128,128]{1,0:T(8,128)S(1)} %get-tuple-element.47), channel_id=1, source_target_pairs={{8,0},{16,8},{24,16},{32,24},{40,32},{48,40},{56,48},{64,56},{72,6... | collective-permute-start | bytes 196616 | tf_op jit(solution)/shard_map/ppermute | solution.py:305
  68.5 4.0 %collective-permute-start.3 = (f32[128,128]{1,0:T(8,128)S(1)}, f32[128,128]{1,0:T(8,128)S(1)}, u32[]{:S(2)}, u32[]{:S(2)}) collective-permute-start(f32[128,128]{1,0:T(8,128)S(1)} %get-tuple-element.48), channel_id=1, source_target_pairs={{0,8},{8,16},{16,24},{24,32},{32,40},{40,48},{48,56},{56,64},{64,7... | collective-permute-start | bytes 196616 | tf_op jit(solution)/shard_map/ppermute | solution.py:304
  72.5 0.4 collective-permute-done.4.for_upper
  72.9 1.0 collective-permute-done.3.for_lower
  73.8 4.9 %all-to-all-done.2 = s16[64,8,128]{2,1,0:T(8,128)(2,1)S(1)} async-done(((s16[64,8,128]{2,1,0:T(8,128)(2,1)}), s16[64,8,128]{2,1,0:T(8,128)(2,1)S(1)}, u32[]{:S(2)}, u32[]{:S(2)}) %all-to-all-start.2) | async-done | bytes 131104 | tf_op jit(solution)/shard_map/all_to_all | solution.py:238
  78.7 0.1 broadcast_in_dim.13
  78.8 9.3 %all_to_all.21.kept = s16[4,512,128]{2,1,0:T(8,128)(2,1)S(1)} all-to-all(s16[4,512,128]{2,1,0:T(8,128)(2,1)S(1)} %broadcast_in_dim.13), channel_id=1, replica_groups=mesh['z'=8,'y'=8,'x'=4,'c'=2] {'x'}, dimensions={0} | all-to-all | bytes 1048576 | tf_op jit(solution)/shard_map/all_to_all | solution.py:238
  88.1 6.8 %collective-permute-start.5 = (s16[4,512,128]{2,1,0:T(8,128)(2,1)S(1)}, s16[4,512,128]{2,1,0:T(8,128)(2,1)S(1)}, u32[]{:S(2)}, u32[]{:S(2)}) collective-permute-start(s16[4,512,128]{2,1,0:T(8,128)(2,1)S(1)} %all_to_all.21.kept), channel_id=1, source_target_pairs={{0,1},{1,0},{2,3},{3,2},{4,5},{5,4},{6,7},{7,6},{8,9},{9,8},{10,11... | collective-permute-start | bytes 1572872 | tf_op jit(solution)/shard_map/ppermute | solution.py:234
  94.9 0.9 finish.1
  95.9 0.6 collective-permute-done.5.received
  96.5 1.6 %whole.1 = f32[3456,128]{1,0:T(8,128)} custom-call(s16[4,512,128]{2,1,0:T(8,128)(2,1)S(1)} %all_to_all.21.kept, s16[4,512,128]{2,1,0:T(8,128)(2,1)S(1)} %collective-permute-done.5.received), custom_call_target="tpu_custom_call" | custom-call | tf_op jit(solution)/shard_map/whole/pallas_call | solution.py:317
  (5 shorter events, 0.0 us)
Async XLA Ops:
  0.6 10.6 %copy-start.2 = (bf16[1,512,128]{2,1,0:T(8,128)(2,1)S(1)}, bf16[1,512,128]{2,1,0:T(8,128)(2,1)}, u32[]{:S(2)}) copy-start(bf16[1,512,128]{2,1,0:T(8,128)(2,1)} %param.11) | copy-start | bytes 393220
  2.6 7.6 %collective-permute-start = (bf16[128,128]{1,0:T(8,128)(2,1)S(1)}, bf16[128,128]{1,0:T(8,128)(2,1)S(1)}, u32[]{:S(2)}, u32[]{:S(2)}) collective-permute-start(bf16[128,128]{1,0:T(8,128)(2,1)S(1)} %get-tuple-element.25), channel_id=1, source_target_pairs={{0,8},{8,16},{16,24},{24,32},{32,40},{40,48},{48,56},{56,64},{64,7... | collective-permute-start | bytes 98312 | tf_op jit(solution)/shard_map/ppermute | solution.py:257
  6.6 4.7 %collective-permute-start.1 = (bf16[128,128]{1,0:T(8,128)(2,1)S(1)}, bf16[128,128]{1,0:T(8,128)(2,1)S(1)}, u32[]{:S(2)}, u32[]{:S(2)}) collective-permute-start(bf16[128,128]{1,0:T(8,128)(2,1)S(1)} %get-tuple-element.26), channel_id=1, source_target_pairs={{8,0},{16,8},{24,16},{32,24},{40,32},{48,40},{56,48},{64,56},{72,6... | collective-permute-start | bytes 98312 | tf_op jit(solution)/shard_map/ppermute | solution.py:258
  10.1 10.5 %copy-start = (bf16[27,128,128]{2,1,0:T(8,128)(2,1)S(1)}, bf16[27,128,128]{2,1,0:T(8,128)(2,1)}, u32[]{:S(2)}) copy-start(bf16[27,128,128]{2,1,0:T(8,128)(2,1)} %weights.5) | copy-start | bytes 2654212
  13.5 9.7 %collective-permute-start.2 = (f32[1728,128]{1,0:T(8,128)S(1)}, f32[1728,128]{1,0:T(8,128)S(1)}, u32[]{:S(2)}, u32[]{:S(2)}) collective-permute-start(f32[1728,128]{1,0:T(8,128)S(1)} %get-tuple-element.29), channel_id=1, source_target_pairs={{0,1},{1,0},{2,3},{3,2},{4,5},{5,4},{6,7},{7,6},{8,9},{9,8},{10,11... | collective-permute-start | bytes 2654216 | tf_op jit(solution)/shard_map/ppermute | solution.py:234
  24.2 12.4 %all-to-all-start = ((s16[4,448,128]{2,1,0:T(8,128)(2,1)}), s16[4,448,128]{2,1,0:T(8,128)(2,1)S(1)}, u32[]{:S(2)}, u32[]{:S(2)}) async-start(s16[4,448,128]{2,1,0:T(8,128)(2,1)} %halves.1), calls=%async_computation | async-start | bytes 917504 | tf_op jit(solution)/shard_map/all_to_all | solution.py:238
  27.8 67.1 %copy-start.1 = (s32[1,2,128]{2,1,0:T(2,128)S(1)}, s32[1,2,128]{2,1,0:T(2,128)}, u32[]{:S(2)}) copy-start(s32[1,2,128]{2,1,0:T(2,128)} %param.9) | copy-start | bytes 3076
  62.5 16.2 %all-to-all-start.2 = ((s16[64,8,128]{2,1,0:T(8,128)(2,1)}), s16[64,8,128]{2,1,0:T(8,128)(2,1)S(1)}, u32[]{:S(2)}, u32[]{:S(2)}) async-start(s16[64,8,128]{2,1,0:T(8,128)(2,1)} %bitcast.7), calls=%async_computation.2 | async-start | bytes 262144 | tf_op jit(solution)/shard_map/all_to_all | solution.py:238
  67.2 5.7 %collective-permute-start.4 = (f32[128,128]{1,0:T(8,128)S(1)}, f32[128,128]{1,0:T(8,128)S(1)}, u32[]{:S(2)}, u32[]{:S(2)}) collective-permute-start(f32[128,128]{1,0:T(8,128)S(1)} %get-tuple-element.47), channel_id=1, source_target_pairs={{8,0},{16,8},{24,16},{32,24},{40,32},{48,40},{56,48},{64,56},{72,6... | collective-permute-start | bytes 196616 | tf_op jit(solution)/shard_map/ppermute | solution.py:305
  68.5 5.4 %collective-permute-start.3 = (f32[128,128]{1,0:T(8,128)S(1)}, f32[128,128]{1,0:T(8,128)S(1)}, u32[]{:S(2)}, u32[]{:S(2)}) collective-permute-start(f32[128,128]{1,0:T(8,128)S(1)} %get-tuple-element.48), channel_id=1, source_target_pairs={{0,8},{8,16},{16,24},{24,32},{32,40},{40,48},{48,56},{56,64},{64,7... | collective-permute-start | bytes 196616 | tf_op jit(solution)/shard_map/ppermute | solution.py:304
  88.1 8.3 %collective-permute-start.5 = (s16[4,512,128]{2,1,0:T(8,128)(2,1)S(1)}, s16[4,512,128]{2,1,0:T(8,128)(2,1)S(1)}, u32[]{:S(2)}, u32[]{:S(2)}) collective-permute-start(s16[4,512,128]{2,1,0:T(8,128)(2,1)S(1)} %all_to_all.21.kept), channel_id=1, source_target_pairs={{0,1},{1,0},{2,3},{3,2},{4,5},{5,4},{6,7},{7,6},{8,9},{9,8},{10,11... | collective-permute-start | bytes 1572872 | tf_op jit(solution)/shard_map/ppermute | solution.py:234

commit v6 on v5

--- a/solution.py
+++ b/solution.py
@@ -169,7 +169,7 @@
     for j, part in enumerate(parts):
         lines[pl.ds(j, PIECES, stride=8), :] = steps(part, exponent)
     lines[pl.ds(7, PIECES, stride=8), :] = exponent.astype(jnp.int32)
-    pieces[...] = lines[...].astype(jnp.int16)
+    pieces[...] = lines[: 8 * PIECES, :].astype(jnp.int16)
 
 
 def pieces_kernel(pieces, spread):
@@ -187,7 +187,7 @@
     copies = []
     for i, (half, place) in enumerate(((kept, core), (received, 1 - core))):
         for q in range(4):
-            lines[4 * i + q] = decode_pieces(half.at[q]).reshape(8 * PIECES, C)
+            lines[4 * i + q, : 8 * PIECES, :] = decode_pieces(half.at[q]).reshape(8 * PIECES, C)
             for j in range(7):
                 start = j * PIECES
                 count = min(PIECES, QUARTER - start)
@@ -293,7 +293,7 @@
         "quarters",
         (quarters,),
         [dealt],
-        [((8 * PIECES, C), jnp.int32)],
+        [((8 * PIECES + 8, C), jnp.int32)],
         scalars=0,
     )
     pieces = exchange(pieces.reshape(PIECES, 8, C), space)
@@ -321,7 +321,7 @@
         out_specs=pl.BlockSpec(memory_space=pl.ANY),
         out_shape=jax.ShapeDtypeStruct((KV * C, C), f32),
         scratch_shapes=[
-            pltpu.VMEM((8, 8 * PIECES, C), f32),
+            pltpu.VMEM((8, 8 * PIECES + 8, C), f32),
             pltpu.VMEM((2, HALF, C), f32),
             pltpu.SemaphoreType.DMA((2,)),
         ],

time: 98.7 us -> 98.7 us (level)
  no operation moved by 1% of the time
where the time goes in v6:
time: 98.7 us; the launch traced here: 98.2 us
  blocking collectives  34.3 us (35%)
  starting transfers between devices  32.9 us (33%)
  Pallas kernels  18.7 us (19%)
  waiting for transfers between devices  10.6 us (11%)
  between operations  1.66 us (2%)
    all_to_all x2, blocking collectives, exchange(): return lax.all_to_all(pieces, axes, 0, 0, tiled=False)  34.3 us
    pallas_call x10, Pallas kernels, call(): pl.pallas_call(kernel, name=name, in_specs=[scalar] * scalars + [operand]...  17.1 us
    ppermute x2, starting transfers between devices, across_c(): return lax.ppermute(part, 'c', [(0, 1), (1, 0)])  14 us
    all_to_all x2, starting transfers between devices, exchange(): return lax.all_to_all(pieces, axes, 0, 0, tiled=False)  8.26 us
    all_to_all x2, waiting for transfers between devices, exchange(): return lax.all_to_all(pieces, axes, 0, 0, tiled=False)  7.53 us
    ppermute x1, starting transfers between devices, per_device(): lower_in = lax.ppermute(to_upper, space, up)  4.03 us
    ppermute x1, starting transfers between devices, per_device(): for_lower = lax.ppermute(ext_grad[VOX + HALO:], space, up)  3.99 us
  transfers between devices with their start and end apart: 8, of which 6 were waited for; matrix products, arithmetic and copies ran while one was open for 0% of the time, Pallas kernels for 12%

profile of v6, /device:TPU:1, one launch (start us, length us, event | category | flops | bytes accessed | tf_op | source)
XLA Modules:
  0.0 98.2 jit_solution(7423147593558140666)
XLA Ops:
  1.3 1.2 %pick.1 = (bf16[128,128]{1,0:T(8,128)(2,1)S(1)}, bf16[128,128]{1,0:T(8,128)(2,1)S(1)}, bf16[128,512]{1,0:T(8,128)(2,1)S(1)}, s32[27,1,512]{2,1,0:T(1,128)S(1)}) custom-call(s32[1,1]{1,0:T(1,128)S(6)} %copy.9.count, bf16[512,128]{1,0:T(8,128)(2,1)} %bitcast.19, s32[2,128]{1,0:T(2,128)} %bitcast.13, s32[27,1,512]{2,1,0:T(1,128)} %bitcast.21), custom_call_target="tpu_custom_call" | custom-call | bytes 439300 | tf_op jit(solution)/shard_map/pick/pallas_call | solution.py:209
  2.6 4.0 %collective-permute-start = (bf16[128,128]{1,0:T(8,128)(2,1)S(1)}, bf16[128,128]{1,0:T(8,128)(2,1)S(1)}, u32[]{:S(2)}, u32[]{:S(2)}) collective-permute-start(bf16[128,128]{1,0:T(8,128)(2,1)S(1)} %get-tuple-element.25), channel_id=1, source_target_pairs={{0,8},{8,16},{16,24},{24,32},{32,40},{40,48},{48,56},{56,64},{64,7... | collective-permute-start | bytes 98312 | tf_op jit(solution)/shard_map/ppermute | solution.py:257
  6.6 1.3 %collective-permute-start.1 = (bf16[128,128]{1,0:T(8,128)(2,1)S(1)}, bf16[128,128]{1,0:T(8,128)(2,1)S(1)}, u32[]{:S(2)}, u32[]{:S(2)}) collective-permute-start(bf16[128,128]{1,0:T(8,128)(2,1)S(1)} %get-tuple-element.26), channel_id=1, source_target_pairs={{8,0},{16,8},{24,16},{32,24},{40,32},{48,40},{56,48},{64,56},{72,6... | collective-permute-start | bytes 98312 | tf_op jit(solution)/shard_map/ppermute | solution.py:258
  7.9 2.2 %local.1.own = bf16[3456,512]{1,0:T(8,128)(2,1)S(1)} custom-call(bf16[128,512]{1,0:T(8,128)(2,1)S(1)} %get-tuple-element.28.table, s32[27,1,512]{2,1,0:T(1,128)S(1)} %get-tuple-element.27.kernel_map), custom_call_target="tpu_custom_call" | custom-call | flops 1811939328 | bytes 3725312 | tf_op jit(solution)/shard_map/local/pallas_call | solution.py:209
  10.1 0.0 copy-start
  10.1 0.0 collective-permute-done.lower
  10.1 1.1 %collective-permute-done.1.upper = bf16[128,128]{1,0:T(8,128)(2,1)S(1)} collective-permute-done((bf16[128,128]{1,0:T(8,128)(2,1)S(1)}, bf16[128,128]{1,0:T(8,128)(2,1)S(1)}, u32[]{:S(2)}, u32[]{:S(2)}) %collective-permute-start.1) | collective-permute-done | bytes 32800 | tf_op jit(solution)/shard_map/ppermute | solution.py:258
  11.3 2.2 %halo.1 = (f32[1728,128]{1,0:T(8,128)S(1)}, f32[1728,128]{1,0:T(8,128)S(1)}, bf16[3456,512]{1,0:T(8,128)(2,1)S(1)}, bf16[512,128]{1,0:T(8,128)(2,1)S(1)}) custom-call(s32[1,1]{1,0:T(1,128)S(6)} %copy.9.count, bf16[128,128]{1,0:T(8,128)(2,1)S(1)} %collective-permute-done.lower, bf16[128,128]{1,0:T(8,128)(2,1)S(1)} %collective-permute-done.1.upper, ...), custom_call_target="tpu_custom_call" | custom-call | flops 1358954496 | bytes 9230340 | tf_op jit(solution)/shard_map/halo/pallas_call | solution.py:209
  13.5 7.2 %collective-permute-start.2 = (f32[1728,128]{1,0:T(8,128)S(1)}, f32[1728,128]{1,0:T(8,128)S(1)}, u32[]{:S(2)}, u32[]{:S(2)}) collective-permute-start(f32[1728,128]{1,0:T(8,128)S(1)} %get-tuple-element.29), channel_id=1, source_target_pairs={{0,1},{1,0},{2,3},{3,2},{4,5},{5,4},{6,7},{7,6},{8,9},{9,8},{10,11... | collective-permute-start | bytes 2654216 | tf_op jit(solution)/shard_map/ppermute | solution.py:234
  20.7 1.4 %output.1 = bf16[512,128]{1,0:T(8,128)(2,1)} custom-call(s32[1,1]{1,0:T(1,128)S(6)} %copy.9.count, bf16[27,128,128]{2,1,0:T(8,128)(2,1)S(1)} %copy-done, bf16[3456,512]{1,0:T(8,128)(2,1)S(1)} %get-tuple-element.31.gathered), custom_call_target="tpu_custom_call" | custom-call | flops 452984832 | bytes 4554756 | tf_op jit(solution)/shard_map/output/pallas_call | solution.py:209
  22.1 1.0 %scatter_first.1.refs_0_ = f32[768,128]{1,0:T(8,128)S(1)} custom-call(bf16[512,128]{1,0:T(8,128)(2,1)S(1)} %get-tuple-element.30.grad_rows, bf16[27,128,128]{2,1,0:T(8,128)(2,1)S(1)} %copy-done, s32[27,1,512]{2,1,0:T(1,128)S(1)} %get-tuple-element.27.kernel_map), custom_call_target="tpu_custom_call" | custom-call | flops 654311424 | bytes 1464320 | tf_op jit(solution)/shard_map/scatter_first/pallas_call | solution.py:209
  23.1 0.0 collective-permute-done.2.received
  23.1 1.0 %halves.1 = s16[4,448,128]{2,1,0:T(8,128)(2,1)} custom-call(f32[1728,128]{1,0:T(8,128)S(1)} %get-tuple-element.33.kept, f32[1728,128]{1,0:T(8,128)S(1)} %collective-permute-done.2.received), custom_call_target="tpu_custom_call" | custom-call | bytes 2228224 | tf_op jit(solution)/shard_map/halves/pallas_call | solution.py:209
  24.2 3.6 %all-to-all-start = ((s16[4,448,128]{2,1,0:T(8,128)(2,1)}), s16[4,448,128]{2,1,0:T(8,128)(2,1)S(1)}, u32[]{:S(2)}, u32[]{:S(2)}) async-start(s16[4,448,128]{2,1,0:T(8,128)(2,1)} %halves.1), calls=%async_computation | async-start | bytes 917504 | tf_op jit(solution)/shard_map/all_to_all | solution.py:238
  27.8 0.0 copy-start.1
  27.8 6.0 %scatter_rest.1.ext_grad = f32[768,128]{1,0:T(8,128)S(1)} custom-call(bf16[512,128]{1,0:T(8,128)(2,1)S(1)} %get-tuple-element.30.grad_rows, bf16[27,128,128]{2,1,0:T(8,128)(2,1)S(1)} %copy-done, s32[27,1,512]{2,1,0:T(1,128)S(1)} %get-tuple-element.27.kernel_map, f32[768,128]{1,0:T(8,128)S(1)} %scatter_first.1.refs_0_), custom_call_target="tpu_custom_call" | custom-call | flops 5234491392 | bytes 1857536 | tf_op jit(solution)/shard_map/scatter_rest/pallas_call | solution.py:209
  33.9 2.7 %all-to-all-done.quarters = s16[4,448,128]{2,1,0:T(8,128)(2,1)S(1)} async-done(((s16[4,448,128]{2,1,0:T(8,128)(2,1)}), s16[4,448,128]{2,1,0:T(8,128)(2,1)S(1)}, u32[]{:S(2)}, u32[]{:S(2)}) %all-to-all-start) | async-done | bytes 458784 | tf_op jit(solution)/shard_map/all_to_all | solution.py:238
  36.5 0.2 quarters.1
  36.8 25.0 %all_to_all.20 = s16[64,8,128]{2,1,0:T(8,128)(2,1)S(1)} all-to-all(s16[64,8,128]{2,1,0:T(8,128)(2,1)S(1)} %bitcast.12), channel_id=1, replica_groups=mesh['z'=8,'y'=8,'x'=4,'c'=2] {'z','y'}, dimensions={0} | all-to-all | bytes 262144 | tf_op jit(solution)/shard_map/all_to_all | solution.py:238
  61.8 0.8 pieces.1
  62.5 4.6 %all-to-all-start.2 = ((s16[64,8,128]{2,1,0:T(8,128)(2,1)}), s16[64,8,128]{2,1,0:T(8,128)(2,1)S(1)}, u32[]{:S(2)}, u32[]{:S(2)}) async-start(s16[64,8,128]{2,1,0:T(8,128)(2,1)} %bitcast.7), calls=%async_computation.2 | async-start | bytes 262144 | tf_op jit(solution)/shard_map/all_to_all | solution.py:238
  67.2 1.3 %collective-permute-start.4 = (f32[128,128]{1,0:T(8,128)S(1)}, f32[128,128]{1,0:T(8,128)S(1)}, u32[]{:S(2)}, u32[]{:S(2)}) collective-permute-start(f32[128,128]{1,0:T(8,128)S(1)} %get-tuple-element.47), channel_id=1, source_target_pairs={{8,0},{16,8},{24,16},{32,24},{40,32},{48,40},{56,48},{64,56},{72,6... | collective-permute-start | bytes 196616 | tf_op jit(solution)/shard_map/ppermute | solution.py:305
  68.5 4.0 %collective-permute-start.3 = (f32[128,128]{1,0:T(8,128)S(1)}, f32[128,128]{1,0:T(8,128)S(1)}, u32[]{:S(2)}, u32[]{:S(2)}) collective-permute-start(f32[128,128]{1,0:T(8,128)S(1)} %get-tuple-element.48), channel_id=1, source_target_pairs={{0,8},{8,16},{16,24},{24,32},{32,40},{40,48},{48,56},{56,64},{64,7... | collective-permute-start | bytes 196616 | tf_op jit(solution)/shard_map/ppermute | solution.py:304
  72.5 0.4 collective-permute-done.4.for_upper
  72.9 1.0 collective-permute-done.3.for_lower
  73.8 4.9 %all-to-all-done.2 = s16[64,8,128]{2,1,0:T(8,128)(2,1)S(1)} async-done(((s16[64,8,128]{2,1,0:T(8,128)(2,1)}), s16[64,8,128]{2,1,0:T(8,128)(2,1)S(1)}, u32[]{:S(2)}, u32[]{:S(2)}) %all-to-all-start.2) | async-done | bytes 131104 | tf_op jit(solution)/shard_map/all_to_all | solution.py:238
  78.7 0.1 broadcast_in_dim.13
  78.8 9.3 %all_to_all.21.kept = s16[4,512,128]{2,1,0:T(8,128)(2,1)S(1)} all-to-all(s16[4,512,128]{2,1,0:T(8,128)(2,1)S(1)} %broadcast_in_dim.13), channel_id=1, replica_groups=mesh['z'=8,'y'=8,'x'=4,'c'=2] {'x'}, dimensions={0} | all-to-all | bytes 1048576 | tf_op jit(solution)/shard_map/all_to_all | solution.py:238
  88.1 6.8 %collective-permute-start.5 = (s16[4,512,128]{2,1,0:T(8,128)(2,1)S(1)}, s16[4,512,128]{2,1,0:T(8,128)(2,1)S(1)}, u32[]{:S(2)}, u32[]{:S(2)}) collective-permute-start(s16[4,512,128]{2,1,0:T(8,128)(2,1)S(1)} %all_to_all.21.kept), channel_id=1, source_target_pairs={{0,1},{1,0},{2,3},{3,2},{4,5},{5,4},{6,7},{7,6},{8,9},{9,8},{10,11... | collective-permute-start | bytes 1572872 | tf_op jit(solution)/shard_map/ppermute | solution.py:234
  94.9 0.9 finish.1
  95.9 0.6 collective-permute-done.5.received
  96.5 1.6 %whole.1 = f32[3456,128]{1,0:T(8,128)} custom-call(s16[4,512,128]{2,1,0:T(8,128)(2,1)S(1)} %all_to_all.21.kept, s16[4,512,128]{2,1,0:T(8,128)(2,1)S(1)} %collective-permute-done.5.received), custom_call_target="tpu_custom_call" | custom-call | tf_op jit(solution)/shard_map/whole/pallas_call | solution.py:317
  (5 shorter events, 0.0 us)
Async XLA Ops:
  0.6 10.6 %copy-start.2 = (bf16[1,512,128]{2,1,0:T(8,128)(2,1)S(1)}, bf16[1,512,128]{2,1,0:T(8,128)(2,1)}, u32[]{:S(2)}) copy-start(bf16[1,512,128]{2,1,0:T(8,128)(2,1)} %param.11) | copy-start | bytes 393220
  2.6 7.6 %collective-permute-start = (bf16[128,128]{1,0:T(8,128)(2,1)S(1)}, bf16[128,128]{1,0:T(8,128)(2,1)S(1)}, u32[]{:S(2)}, u32[]{:S(2)}) collective-permute-start(bf16[128,128]{1,0:T(8,128)(2,1)S(1)} %get-tuple-element.25), channel_id=1, source_target_pairs={{0,8},{8,16},{16,24},{24,32},{32,40},{40,48},{48,56},{56,64},{64,7... | collective-permute-start | bytes 98312 | tf_op jit(solution)/shard_map/ppermute | solution.py:257
  6.6 4.7 %collective-permute-start.1 = (bf16[128,128]{1,0:T(8,128)(2,1)S(1)}, bf16[128,128]{1,0:T(8,128)(2,1)S(1)}, u32[]{:S(2)}, u32[]{:S(2)}) collective-permute-start(bf16[128,128]{1,0:T(8,128)(2,1)S(1)} %get-tuple-element.26), channel_id=1, source_target_pairs={{8,0},{16,8},{24,16},{32,24},{40,32},{48,40},{56,48},{64,56},{72,6... | collective-permute-start | bytes 98312 | tf_op jit(solution)/shard_map/ppermute | solution.py:258
  10.1 10.5 %copy-start = (bf16[27,128,128]{2,1,0:T(8,128)(2,1)S(1)}, bf16[27,128,128]{2,1,0:T(8,128)(2,1)}, u32[]{:S(2)}) copy-start(bf16[27,128,128]{2,1,0:T(8,128)(2,1)} %weights.5) | copy-start | bytes 2654212
  13.5 9.7 %collective-permute-start.2 = (f32[1728,128]{1,0:T(8,128)S(1)}, f32[1728,128]{1,0:T(8,128)S(1)}, u32[]{:S(2)}, u32[]{:S(2)}) collective-permute-start(f32[1728,128]{1,0:T(8,128)S(1)} %get-tuple-element.29), channel_id=1, source_target_pairs={{0,1},{1,0},{2,3},{3,2},{4,5},{5,4},{6,7},{7,6},{8,9},{9,8},{10,11... | collective-permute-start | bytes 2654216 | tf_op jit(solution)/shard_map/ppermute | solution.py:234
  24.2 12.4 %all-to-all-start = ((s16[4,448,128]{2,1,0:T(8,128)(2,1)}), s16[4,448,128]{2,1,0:T(8,128)(2,1)S(1)}, u32[]{:S(2)}, u32[]{:S(2)}) async-start(s16[4,448,128]{2,1,0:T(8,128)(2,1)} %halves.1), calls=%async_computation | async-start | bytes 917504 | tf_op jit(solution)/shard_map/all_to_all | solution.py:238
  27.8 67.1 %copy-start.1 = (s32[1,2,128]{2,1,0:T(2,128)S(1)}, s32[1,2,128]{2,1,0:T(2,128)}, u32[]{:S(2)}) copy-start(s32[1,2,128]{2,1,0:T(2,128)} %param.9) | copy-start | bytes 3076
  62.5 16.2 %all-to-all-start.2 = ((s16[64,8,128]{2,1,0:T(8,128)(2,1)}), s16[64,8,128]{2,1,0:T(8,128)(2,1)S(1)}, u32[]{:S(2)}, u32[]{:S(2)}) async-start(s16[64,8,128]{2,1,0:T(8,128)(2,1)} %bitcast.7), calls=%async_computation.2 | async-start | bytes 262144 | tf_op jit(solution)/shard_map/all_to_all | solution.py:238
  67.2 5.7 %collective-permute-start.4 = (f32[128,128]{1,0:T(8,128)S(1)}, f32[128,128]{1,0:T(8,128)S(1)}, u32[]{:S(2)}, u32[]{:S(2)}) collective-permute-start(f32[128,128]{1,0:T(8,128)S(1)} %get-tuple-element.47), channel_id=1, source_target_pairs={{8,0},{16,8},{24,16},{32,24},{40,32},{48,40},{56,48},{64,56},{72,6... | collective-permute-start | bytes 196616 | tf_op jit(solution)/shard_map/ppermute | solution.py:305
  68.5 5.4 %collective-permute-start.3 = (f32[128,128]{1,0:T(8,128)S(1)}, f32[128,128]{1,0:T(8,128)S(1)}, u32[]{:S(2)}, u32[]{:S(2)}) collective-permute-start(f32[128,128]{1,0:T(8,128)S(1)} %get-tuple-element.48), channel_id=1, source_target_pairs={{0,8},{8,16},{16,24},{24,32},{32,40},{40,48},{48,56},{56,64},{64,7... | collective-permute-start | bytes 196616 | tf_op jit(solution)/shard_map/ppermute | solution.py:304
  88.1 8.3 %collective-permute-start.5 = (s16[4,512,128]{2,1,0:T(8,128)(2,1)S(1)}, s16[4,512,128]{2,1,0:T(8,128)(2,1)S(1)}, u32[]{:S(2)}, u32[]{:S(2)}) collective-permute-start(s16[4,512,128]{2,1,0:T(8,128)(2,1)S(1)} %all_to_all.21.kept), channel_id=1, source_target_pairs={{0,1},{1,0},{2,3},{3,2},{4,5},{5,4},{6,7},{7,6},{8,9},{9,8},{10,11... | collective-permute-start | bytes 1572872 | tf_op jit(solution)/shard_map/ppermute | solution.py:234

commit v7 on v6

--- a/solution.py
+++ b/solution.py
@@ -102,9 +102,10 @@
     *earlier, ext_grad, contribs = refs
     for first in range(*offsets, GROUP):
         group = range(first, first + GROUP)
-        for j, k in enumerate(group):
-            contrib = matmul(grad_rows[...], weights[k], ((1,), (1,)))
-            contribs[j * VOX : (j + 1) * VOX, :] = split(contrib)
+        side = weights[first : first + GROUP].reshape(GROUP * C, C)
+        contrib = matmul(grad_rows[...], side, ((1,), (1,)))
+        for j in range(GROUP):
+            contribs[j * VOX : (j + 1) * VOX, :] = split(contrib[:, j * C : (j + 1) * C])
         for row in range(0, EXT, TILE):
             rows = [offset_onehot(kernel_map, k, TILE, row) for k in group]
             part = joined(matmul(jnp.concatenate(rows, axis=1), contribs[...]))

time: 98.7 us -> 98.8 us (level)
  no operation moved by 1% of the time
where the time goes in v7:
time: 98.8 us; the launch traced here: 98.3 us
  blocking collectives  34.3 us (35%)
  starting transfers between devices  32.9 us (33%)
  Pallas kernels  18.8 us (19%)
  waiting for transfers between devices  10.6 us (11%)
  between operations  1.66 us (2%)
    all_to_all x2, blocking collectives, exchange(): return lax.all_to_all(pieces, axes, 0, 0, tiled=False)  34.3 us
    pallas_call x10, Pallas kernels, call(): pl.pallas_call(kernel, name=name, in_specs=[scalar] * scalars + [operand]...  17.2 us
    ppermute x2, starting transfers between devices, across_c(): return lax.ppermute(part, 'c', [(0, 1), (1, 0)])  14 us
    all_to_all x2, starting transfers between devices, exchange(): return lax.all_to_all(pieces, axes, 0, 0, tiled=False)  8.26 us
    all_to_all x2, waiting for transfers between devices, exchange(): return lax.all_to_all(pieces, axes, 0, 0, tiled=False)  7.5 us
    ppermute x1, starting transfers between devices, per_device(): lower_in = lax.ppermute(to_upper, space, up)  4.03 us
    ppermute x1, starting transfers between devices, per_device(): for_lower = lax.ppermute(ext_grad[VOX + HALO:], space, up)  3.99 us
  transfers between devices with their start and end apart: 8, of which 6 were waited for; matrix products, arithmetic and copies ran while one was open for 0% of the time, Pallas kernels for 12%

profile of v7, /device:TPU:1, one launch (start us, length us, event | category | flops | bytes accessed | tf_op | source)
XLA Modules:
  0.0 98.3 jit_solution(10251019243774535628)
XLA Ops:
  1.3 1.2 %pick.1 = (bf16[128,128]{1,0:T(8,128)(2,1)S(1)}, bf16[128,128]{1,0:T(8,128)(2,1)S(1)}, bf16[128,512]{1,0:T(8,128)(2,1)S(1)}, s32[27,1,512]{2,1,0:T(1,128)S(1)}) custom-call(s32[1,1]{1,0:T(1,128)S(6)} %copy.9.count, bf16[512,128]{1,0:T(8,128)(2,1)} %bitcast.19, s32[2,128]{1,0:T(2,128)} %bitcast.13, s32[27,1,512]{2,1,0:T(1,128)} %bitcast.21), custom_call_target="tpu_custom_call" | custom-call | bytes 439300 | tf_op jit(solution)/shard_map/pick/pallas_call | solution.py:210
  2.6 4.0 %collective-permute-start = (bf16[128,128]{1,0:T(8,128)(2,1)S(1)}, bf16[128,128]{1,0:T(8,128)(2,1)S(1)}, u32[]{:S(2)}, u32[]{:S(2)}) collective-permute-start(bf16[128,128]{1,0:T(8,128)(2,1)S(1)} %get-tuple-element.25), channel_id=1, source_target_pairs={{0,8},{8,16},{16,24},{24,32},{32,40},{40,48},{48,56},{56,64},{64,7... | collective-permute-start | bytes 98312 | tf_op jit(solution)/shard_map/ppermute | solution.py:258
  6.6 1.3 %collective-permute-start.1 = (bf16[128,128]{1,0:T(8,128)(2,1)S(1)}, bf16[128,128]{1,0:T(8,128)(2,1)S(1)}, u32[]{:S(2)}, u32[]{:S(2)}) collective-permute-start(bf16[128,128]{1,0:T(8,128)(2,1)S(1)} %get-tuple-element.26), channel_id=1, source_target_pairs={{8,0},{16,8},{24,16},{32,24},{40,32},{48,40},{56,48},{64,56},{72,6... | collective-permute-start | bytes 98312 | tf_op jit(solution)/shard_map/ppermute | solution.py:259
  7.9 2.2 %local.1.own = bf16[3456,512]{1,0:T(8,128)(2,1)S(1)} custom-call(bf16[128,512]{1,0:T(8,128)(2,1)S(1)} %get-tuple-element.28.table, s32[27,1,512]{2,1,0:T(1,128)S(1)} %get-tuple-element.27.kernel_map), custom_call_target="tpu_custom_call" | custom-call | flops 1811939328 | bytes 3725312 | tf_op jit(solution)/shard_map/local/pallas_call | solution.py:210
  10.1 0.0 copy-start
  10.1 0.0 collective-permute-done.lower
  10.1 1.1 %collective-permute-done.1.upper = bf16[128,128]{1,0:T(8,128)(2,1)S(1)} collective-permute-done((bf16[128,128]{1,0:T(8,128)(2,1)S(1)}, bf16[128,128]{1,0:T(8,128)(2,1)S(1)}, u32[]{:S(2)}, u32[]{:S(2)}) %collective-permute-start.1) | collective-permute-done | bytes 32800 | tf_op jit(solution)/shard_map/ppermute | solution.py:259
  11.3 2.2 %halo.1 = (f32[1728,128]{1,0:T(8,128)S(1)}, f32[1728,128]{1,0:T(8,128)S(1)}, bf16[3456,512]{1,0:T(8,128)(2,1)S(1)}, bf16[512,128]{1,0:T(8,128)(2,1)S(1)}) custom-call(s32[1,1]{1,0:T(1,128)S(6)} %copy.9.count, bf16[128,128]{1,0:T(8,128)(2,1)S(1)} %collective-permute-done.lower, bf16[128,128]{1,0:T(8,128)(2,1)S(1)} %collective-permute-done.1.upper, ...), custom_call_target="tpu_custom_call" | custom-call | flops 1358954496 | bytes 9230340 | tf_op jit(solution)/shard_map/halo/pallas_call | solution.py:210
  13.5 7.2 %collective-permute-start.2 = (f32[1728,128]{1,0:T(8,128)S(1)}, f32[1728,128]{1,0:T(8,128)S(1)}, u32[]{:S(2)}, u32[]{:S(2)}) collective-permute-start(f32[1728,128]{1,0:T(8,128)S(1)} %get-tuple-element.29), channel_id=1, source_target_pairs={{0,1},{1,0},{2,3},{3,2},{4,5},{5,4},{6,7},{7,6},{8,9},{9,8},{10,11... | collective-permute-start | bytes 2654216 | tf_op jit(solution)/shard_map/ppermute | solution.py:235
  20.7 1.4 %output.1 = bf16[512,128]{1,0:T(8,128)(2,1)} custom-call(s32[1,1]{1,0:T(1,128)S(6)} %copy.9.count, bf16[27,128,128]{2,1,0:T(8,128)(2,1)S(1)} %copy-done, bf16[3456,512]{1,0:T(8,128)(2,1)S(1)} %get-tuple-element.31.gathered), custom_call_target="tpu_custom_call" | custom-call | flops 452984832 | bytes 4554756 | tf_op jit(solution)/shard_map/output/pallas_call | solution.py:210
  22.1 1.1 %scatter_first.1.refs_0_ = f32[768,128]{1,0:T(8,128)S(1)} custom-call(bf16[512,128]{1,0:T(8,128)(2,1)S(1)} %get-tuple-element.30.grad_rows, bf16[27,128,128]{2,1,0:T(8,128)(2,1)S(1)} %copy-done, s32[27,1,512]{2,1,0:T(1,128)S(1)} %get-tuple-element.27.kernel_map), custom_call_target="tpu_custom_call" | custom-call | flops 654311424 | bytes 1464320 | tf_op jit(solution)/shard_map/scatter_first/pallas_call | solution.py:210
  23.2 0.0 collective-permute-done.2.received
  23.2 1.0 %halves.1 = s16[4,448,128]{2,1,0:T(8,128)(2,1)} custom-call(f32[1728,128]{1,0:T(8,128)S(1)} %get-tuple-element.33.kept, f32[1728,128]{1,0:T(8,128)S(1)} %collective-permute-done.2.received), custom_call_target="tpu_custom_call" | custom-call | bytes 2228224 | tf_op jit(solution)/shard_map/halves/pallas_call | solution.py:210
  24.2 3.6 %all-to-all-start = ((s16[4,448,128]{2,1,0:T(8,128)(2,1)}), s16[4,448,128]{2,1,0:T(8,128)(2,1)S(1)}, u32[]{:S(2)}, u32[]{:S(2)}) async-start(s16[4,448,128]{2,1,0:T(8,128)(2,1)} %halves.1), calls=%async_computation | async-start | bytes 917504 | tf_op jit(solution)/shard_map/all_to_all | solution.py:239
  27.9 0.0 copy-start.1
  27.9 6.1 %scatter_rest.1.ext_grad = f32[768,128]{1,0:T(8,128)S(1)} custom-call(bf16[512,128]{1,0:T(8,128)(2,1)S(1)} %get-tuple-element.30.grad_rows, bf16[27,128,128]{2,1,0:T(8,128)(2,1)S(1)} %copy-done, s32[27,1,512]{2,1,0:T(1,128)S(1)} %get-tuple-element.27.kernel_map, f32[768,128]{1,0:T(8,128)S(1)} %scatter_first.1.refs_0_), custom_call_target="tpu_custom_call" | custom-call | flops 5234491392 | bytes 1857536 | tf_op jit(solution)/shard_map/scatter_rest/pallas_call | solution.py:210
  34.0 2.6 %all-to-all-done.quarters = s16[4,448,128]{2,1,0:T(8,128)(2,1)S(1)} async-done(((s16[4,448,128]{2,1,0:T(8,128)(2,1)}), s16[4,448,128]{2,1,0:T(8,128)(2,1)S(1)}, u32[]{:S(2)}, u32[]{:S(2)}) %all-to-all-start) | async-done | bytes 458784 | tf_op jit(solution)/shard_map/all_to_all | solution.py:239
  36.6 0.2 quarters.1
  36.9 25.0 %all_to_all.20 = s16[64,8,128]{2,1,0:T(8,128)(2,1)S(1)} all-to-all(s16[64,8,128]{2,1,0:T(8,128)(2,1)S(1)} %bitcast.12), channel_id=1, replica_groups=mesh['z'=8,'y'=8,'x'=4,'c'=2] {'z','y'}, dimensions={0} | all-to-all | bytes 262144 | tf_op jit(solution)/shard_map/all_to_all | solution.py:239
  61.8 0.8 pieces.1
  62.6 4.6 %all-to-all-start.2 = ((s16[64,8,128]{2,1,0:T(8,128)(2,1)}), s16[64,8,128]{2,1,0:T(8,128)(2,1)S(1)}, u32[]{:S(2)}, u32[]{:S(2)}) async-start(s16[64,8,128]{2,1,0:T(8,128)(2,1)} %bitcast.7), calls=%async_computation.2 | async-start | bytes 262144 | tf_op jit(solution)/shard_map/all_to_all | solution.py:239
  67.2 1.3 %collective-permute-start.4 = (f32[128,128]{1,0:T(8,128)S(1)}, f32[128,128]{1,0:T(8,128)S(1)}, u32[]{:S(2)}, u32[]{:S(2)}) collective-permute-start(f32[128,128]{1,0:T(8,128)S(1)} %get-tuple-element.47), channel_id=1, source_target_pairs={{8,0},{16,8},{24,16},{32,24},{40,32},{48,40},{56,48},{64,56},{72,6... | collective-permute-start | bytes 196616 | tf_op jit(solution)/shard_map/ppermute | solution.py:306
  68.5 4.0 %collective-permute-start.3 = (f32[128,128]{1,0:T(8,128)S(1)}, f32[128,128]{1,0:T(8,128)S(1)}, u32[]{:S(2)}, u32[]{:S(2)}) collective-permute-start(f32[128,128]{1,0:T(8,128)S(1)} %get-tuple-element.48), channel_id=1, source_target_pairs={{0,8},{8,16},{16,24},{24,32},{32,40},{40,48},{48,56},{56,64},{64,7... | collective-permute-start | bytes 196616 | tf_op jit(solution)/shard_map/ppermute | solution.py:305
  72.5 0.4 collective-permute-done.4.for_upper
  72.9 1.0 collective-permute-done.3.for_lower
  73.9 4.9 %all-to-all-done.2 = s16[64,8,128]{2,1,0:T(8,128)(2,1)S(1)} async-done(((s16[64,8,128]{2,1,0:T(8,128)(2,1)}), s16[64,8,128]{2,1,0:T(8,128)(2,1)S(1)}, u32[]{:S(2)}, u32[]{:S(2)}) %all-to-all-start.2) | async-done | bytes 131104 | tf_op jit(solution)/shard_map/all_to_all | solution.py:239
  78.8 0.1 broadcast_in_dim.13
  78.8 9.3 %all_to_all.21.kept = s16[4,512,128]{2,1,0:T(8,128)(2,1)S(1)} all-to-all(s16[4,512,128]{2,1,0:T(8,128)(2,1)S(1)} %broadcast_in_dim.13), channel_id=1, replica_groups=mesh['z'=8,'y'=8,'x'=4,'c'=2] {'x'}, dimensions={0} | all-to-all | bytes 1048576 | tf_op jit(solution)/shard_map/all_to_all | solution.py:239
  88.2 6.8 %collective-permute-start.5 = (s16[4,512,128]{2,1,0:T(8,128)(2,1)S(1)}, s16[4,512,128]{2,1,0:T(8,128)(2,1)S(1)}, u32[]{:S(2)}, u32[]{:S(2)}) collective-permute-start(s16[4,512,128]{2,1,0:T(8,128)(2,1)S(1)} %all_to_all.21.kept), channel_id=1, source_target_pairs={{0,1},{1,0},{2,3},{3,2},{4,5},{5,4},{6,7},{7,6},{8,9},{9,8},{10,11... | collective-permute-start | bytes 1572872 | tf_op jit(solution)/shard_map/ppermute | solution.py:235
  95.0 0.9 finish.1
  96.0 0.6 collective-permute-done.5.received
  96.5 1.6 %whole.1 = f32[3456,128]{1,0:T(8,128)} custom-call(s16[4,512,128]{2,1,0:T(8,128)(2,1)S(1)} %all_to_all.21.kept, s16[4,512,128]{2,1,0:T(8,128)(2,1)S(1)} %collective-permute-done.5.received), custom_call_target="tpu_custom_call" | custom-call | tf_op jit(solution)/shard_map/whole/pallas_call | solution.py:318
  (5 shorter events, 0.0 us)
Async XLA Ops:
  0.6 10.6 %copy-start.2 = (bf16[1,512,128]{2,1,0:T(8,128)(2,1)S(1)}, bf16[1,512,128]{2,1,0:T(8,128)(2,1)}, u32[]{:S(2)}) copy-start(bf16[1,512,128]{2,1,0:T(8,128)(2,1)} %param.11) | copy-start | bytes 393220
  2.6 7.6 %collective-permute-start = (bf16[128,128]{1,0:T(8,128)(2,1)S(1)}, bf16[128,128]{1,0:T(8,128)(2,1)S(1)}, u32[]{:S(2)}, u32[]{:S(2)}) collective-permute-start(bf16[128,128]{1,0:T(8,128)(2,1)S(1)} %get-tuple-element.25), channel_id=1, source_target_pairs={{0,8},{8,16},{16,24},{24,32},{32,40},{40,48},{48,56},{56,64},{64,7... | collective-permute-start | bytes 98312 | tf_op jit(solution)/shard_map/ppermute | solution.py:258
  6.6 4.7 %collective-permute-start.1 = (bf16[128,128]{1,0:T(8,128)(2,1)S(1)}, bf16[128,128]{1,0:T(8,128)(2,1)S(1)}, u32[]{:S(2)}, u32[]{:S(2)}) collective-permute-start(bf16[128,128]{1,0:T(8,128)(2,1)S(1)} %get-tuple-element.26), channel_id=1, source_target_pairs={{8,0},{16,8},{24,16},{32,24},{40,32},{48,40},{56,48},{64,56},{72,6... | collective-permute-start | bytes 98312 | tf_op jit(solution)/shard_map/ppermute | solution.py:259
  10.1 10.5 %copy-start = (bf16[27,128,128]{2,1,0:T(8,128)(2,1)S(1)}, bf16[27,128,128]{2,1,0:T(8,128)(2,1)}, u32[]{:S(2)}) copy-start(bf16[27,128,128]{2,1,0:T(8,128)(2,1)} %weights.5) | copy-start | bytes 2654212
  13.5 9.7 %collective-permute-start.2 = (f32[1728,128]{1,0:T(8,128)S(1)}, f32[1728,128]{1,0:T(8,128)S(1)}, u32[]{:S(2)}, u32[]{:S(2)}) collective-permute-start(f32[1728,128]{1,0:T(8,128)S(1)} %get-tuple-element.29), channel_id=1, source_target_pairs={{0,1},{1,0},{2,3},{3,2},{4,5},{5,4},{6,7},{7,6},{8,9},{9,8},{10,11... | collective-permute-start | bytes 2654216 | tf_op jit(solution)/shard_map/ppermute | solution.py:235
  24.2 12.4 %all-to-all-start = ((s16[4,448,128]{2,1,0:T(8,128)(2,1)}), s16[4,448,128]{2,1,0:T(8,128)(2,1)S(1)}, u32[]{:S(2)}, u32[]{:S(2)}) async-start(s16[4,448,128]{2,1,0:T(8,128)(2,1)} %halves.1), calls=%async_computation | async-start | bytes 917504 | tf_op jit(solution)/shard_map/all_to_all | solution.py:239
  27.9 67.1 %copy-start.1 = (s32[1,2,128]{2,1,0:T(2,128)S(1)}, s32[1,2,128]{2,1,0:T(2,128)}, u32[]{:S(2)}) copy-start(s32[1,2,128]{2,1,0:T(2,128)} %param.9) | copy-start | bytes 3076
  62.6 16.2 %all-to-all-start.2 = ((s16[64,8,128]{2,1,0:T(8,128)(2,1)}), s16[64,8,128]{2,1,0:T(8,128)(2,1)S(1)}, u32[]{:S(2)}, u32[]{:S(2)}) async-start(s16[64,8,128]{2,1,0:T(8,128)(2,1)} %bitcast.7), calls=%async_computation.2 | async-start | bytes 262144 | tf_op jit(solution)/shard_map/all_to_all | solution.py:239
  67.2 5.7 %collective-permute-start.4 = (f32[128,128]{1,0:T(8,128)S(1)}, f32[128,128]{1,0:T(8,128)S(1)}, u32[]{:S(2)}, u32[]{:S(2)}) collective-permute-start(f32[128,128]{1,0:T(8,128)S(1)} %get-tuple-element.47), channel_id=1, source_target_pairs={{8,0},{16,8},{24,16},{32,24},{40,32},{48,40},{56,48},{64,56},{72,6... | collective-permute-start | bytes 196616 | tf_op jit(solution)/shard_map/ppermute | solution.py:306
  68.5 5.4 %collective-permute-start.3 = (f32[128,128]{1,0:T(8,128)S(1)}, f32[128,128]{1,0:T(8,128)S(1)}, u32[]{:S(2)}, u32[]{:S(2)}) collective-permute-start(f32[128,128]{1,0:T(8,128)S(1)} %get-tuple-element.48), channel_id=1, source_target_pairs={{0,8},{8,16},{16,24},{24,32},{32,40},{40,48},{48,56},{56,64},{64,7... | collective-permute-start | bytes 196616 | tf_op jit(solution)/shard_map/ppermute | solution.py:305
  88.2 8.3 %collective-permute-start.5 = (s16[4,512,128]{2,1,0:T(8,128)(2,1)S(1)}, s16[4,512,128]{2,1,0:T(8,128)(2,1)S(1)}, u32[]{:S(2)}, u32[]{:S(2)}) collective-permute-start(s16[4,512,128]{2,1,0:T(8,128)(2,1)S(1)} %all_to_all.21.kept), channel_id=1, source_target_pairs={{0,1},{1,0},{2,3},{3,2},{4,5},{5,4},{6,7},{7,6},{8,9},{9,8},{10,11... | collective-permute-start | bytes 1572872 | tf_op jit(solution)/shard_map/ppermute | solution.py:235
